TPU v7x, 256 devices: a whole 4x4x8 slice. The times are simulated.
256 devices in a mesh: dp: 32 (over z, y), tensor: 8 (over x, core).
Axes of the slice: x: 4, y: 4, z: 8, core: 2. Of those that a mesh axis runs over, the one named last changes fastest.
Arguments:
- hidden: bfloat16 [4096, 26624], P('dp', 'tensor'), may hold values from -6 to 6
- out_grad: bfloat16 [4096, 8192], P(('dp', 'tensor')), may hold values from -0.375 to 0.375
- master: float32 [8192, 26624], P('dp', 'tensor'), may hold values from -0.3125 to 0.3125
- first_moment: bfloat16 [8192, 26624], P('dp', 'tensor'), may hold values from -4 to 4
- second_moment: bfloat16 [8192, 26624], P('dp', 'tensor'), may hold values from 0.049804688 to 1
- row_counts: int32 [8], replicated, may hold values from 2816 to 3840, as said below
- step_count: int32 [1], replicated, may hold values from 1 to 11
Outputs:
- adam_update: float32 [8192, 26624], P('dp', 'tensor')
- weights_tp: bfloat16 [8192, 30720], P('dp', 'tensor')
Inputs may be any that keep to these rules, and one draw needn't show every extreme that they name: Tensor index j takes row_counts[j] consecutive hidden units in order; they sum to 26624; offsets[j] differs from j * 3328 by at most 256; the largest count equals 3840.
All inputs are finite; a program needn't handle non-finite values.
Results may differ from a plain program's by a relative error of at most 0.0045.
Values may be sent and summed in bfloat16 or wider, within the bound.
No kernel may reach another device: no remote copies, remote signals or barrier semaphores. Data moves between devices by JAX's collectives and lax.ppermute only.
A program may use at most 192 MiB of HBM per device.

v0:
```python
import math

import jax
import jax.numpy as jnp
from jax import lax
from jax.sharding import PartitionSpec as P

DRIFT = 256
CAP = 3840


beta_first = 0.9
beta_second = 0.95
epsilon = 1e-08
decay_rate = 0.1
learn_rate = 0.001


def extended(cells, sides, width):
    for axis, dim in sides:
        count = lax.axis_size(axis)
        ends = count - 1
        head = lax.slice_in_dim(cells, 0, width, axis=dim)
        tail = lax.slice_in_dim(cells, cells.shape[dim] - width, cells.shape[dim], axis=dim)
        cells = jnp.concatenate(
            [
                lax.ppermute(tail, axis, [(i, (i + 1) % count) for i in range(ends)]),
                cells,
                lax.ppermute(head, axis, [((i + 1) % count, i) for i in range(ends)]),
            ],
            axis=dim,
        )
    return cells


def adamw(gradient, master, first_moment, second_moment, steps_done):
    first_new = beta_first * first_moment + (1.0 - beta_first) * gradient
    second_new = beta_second * second_moment + (1.0 - beta_second) * gradient * gradient
    first_fix = 1.0 - jnp.power(beta_first, steps_done)
    second_fix = 1.0 - jnp.power(beta_second, steps_done)
    update = (
        first_new / first_fix / (jnp.sqrt(second_new / second_fix) + epsilon) + decay_rate * master
    )
    master_new = master - learn_rate * update
    return (master_new, update)


def relayout(weights, row_counts):
    shard_rows = weights.shape[0]
    shard_width = weights.shape[1]
    offsets = jnp.cumsum(row_counts) - row_counts
    position = lax.axis_index("tensor")
    first_slot = lax.dynamic_index_in_dim(offsets, position, keepdims=False)
    length = lax.dynamic_index_in_dim(row_counts, position, keepdims=False)
    padded = extended(weights, (("tensor", 1),), DRIFT)
    widened = jnp.concatenate([padded, jnp.zeros((shard_rows, 2 * DRIFT), jnp.bfloat16)], axis=1)
    start = first_slot - position * shard_width + DRIFT
    window = lax.dynamic_slice_in_dim(widened, start, CAP, 1)
    slot_index = jnp.arange(CAP, dtype=jnp.int32)
    return jnp.where((slot_index < length)[None, :], window, jnp.zeros((), jnp.bfloat16))


def per_device(hidden, out_grad, master, first_moment, second_moment, row_counts, step_count):
    shard_rows = master.shape[0]
    hidden_units = hidden.shape[1]
    regrouped = lax.all_to_all(out_grad, "dp", split_axis=1, concat_axis=0, tiled=True)
    spread = lax.all_gather(regrouped, "tensor", axis=0, tiled=True)
    tensor_count = lax.axis_size("tensor")
    data_count = lax.axis_size("dp")
    local_tokens = out_grad.shape[0]
    group_tokens = hidden.shape[0]
    owned_cols = spread.reshape(tensor_count, data_count, local_tokens, shard_rows)
    shard_piece = lax.all_gather(hidden, "dp", axis=0, tiled=True)
    groups = shard_piece.shape[0] // group_tokens
    per_turn = math.gcd(groups, 4)
    turns = groups // per_turn
    activations = shard_piece.reshape(groups, tensor_count, local_tokens, hidden_units)

    def one_turn(turn_index, running):
        grad_block = lax.dynamic_slice_in_dim(owned_cols, turn_index * per_turn, per_turn, 1)
        act_block = lax.dynamic_slice_in_dim(activations, turn_index * per_turn, per_turn, 0)
        partial_value = jnp.einsum(
            "tgrd,gtrf->gdf", grad_block, act_block, preferred_element_type=jnp.float32
        )
        rounded = lax.optimization_barrier(partial_value.astype(jnp.bfloat16)).astype(jnp.float32)
        return running + jnp.sum(rounded, axis=0)

    gradient = lax.fori_loop(0, turns, one_turn, jnp.zeros((shard_rows, hidden_units), jnp.float32))
    steps_done = step_count[0].astype(jnp.float32)
    master_new, update = adamw(
        gradient,
        master,
        first_moment.astype(jnp.float32),
        second_moment.astype(jnp.float32),
        steps_done,
    )
    laid = relayout(master_new.astype(jnp.bfloat16), row_counts)
    outputs = [(update, laid)]
    joined = [jnp.concatenate([entry[slot] for entry in outputs], axis=0) for slot in range(2)]
    return (joined[0], joined[1])


def solution(mesh):
    return jax.shard_map(
        per_device,
        mesh=mesh,
        in_specs=(
            P("dp", "tensor"),
            P(("dp", "tensor"), None),
            P("dp", "tensor"),
            P("dp", "tensor"),
            P("dp", "tensor"),
            P(),
            P(),
        ),
        out_specs=(P("dp", "tensor"), P("dp", "tensor")),
        check_vma=False,
    )
```

profile of v0, /device:TPU:1, one launch (start us, length us, event | category | flops | bytes accessed | tf_op | source)
XLA Modules:
  0.0 353.1 jit_solution(3971043392902554566)
XLA Ops:
  7.2 0.0 all-gather.3.cloned.1.call-start
  7.2 1.0 copy.20
  8.2 23.1 %all_to_all.19 = bf16[16,32,256]{2,0,1:T(8,128)(2,1)} all-to-all(bf16[16,32,256]{2,0,1:T(8,128)(2,1)S(1)} %bitcast.22), channel_id=1, replica_groups=mesh['dp'=32,'tensor'=8] {'dp'}, dimensions={1} | all-to-all | bytes 524288 | tf_op jit(solution)/shard_map/all_to_all | solution.py:66
  31.3 0.0 all-gather.3.cloned.1.call-update
  31.3 0.0 all-gather.5.cloned.1.call-start
  31.4 0.7 all-gather.5.cloned.1.call-update
  32.8 0.8 reduce-window.9
  33.7 1.2 dynamic_slice.24
  34.9 0.7 bitcast_subtract_fusion
  35.6 21.4 %all-gather.3.cloned.1.call-done = bf16[4096,256]{1,0:T(8,128)(2,1)} async-done(((bf16[512,256]{1,0:T(8,128)(2,1)}), bf16[4096,256]{1,0:T(8,128)(2,1)}) %all-gather.3.cloned.1.call-update) | async-done | bytes 2097168 | tf_op jit(solution)/shard_map/all_gather | solution.py:67
  56.9 198.3 %all-gather.5.cloned.1.call-done = bf16[4096,3328]{1,0:T(8,128)(2,1)} async-done(((bf16[128,3328]{1,0:T(8,128)(2,1)}), bf16[4096,3328]{1,0:T(8,128)(2,1)}) %all-gather.5.cloned.1.call-update) | async-done | bytes 27262992 | tf_op jit(solution)/shard_map/all_gather | solution.py:73
  255.3 71.0 %while.14 = (s32[]{:T(128)}, f32[256,3328]{1,0:T(8,128)}, bf16[8,32,16,256]{3,2,1,0:T(8,128)(2,1)}, bf16[32,8,16,3328]{3,2,1,0:T(8,128)(2,1)}, s32[]{:T(128)}, /*index=5*/s32[]{:T(128)}, s32[]{:T(128)}, s32[]{:T(128)}) while((s32[]{:T(128)}, f32[256,3328]{1,0:T(8,128)}, bf16[8,32,16,256]{3,2,1,0:T(8,128)(2,1)}, ...), condition=%wide.region_2.0_spmd.clone, body=%wide.region_0.0_spmd.clone.sunk | while | flops 883490816 | bytes 30934164 | solution.py:88
  255.3 4.0 %bitcast_convert_fusion.2 = bf16[4,256,3328]{2,1,0:T(8,128)(2,1)S(1)} fusion(bf16[32,8,16,3328]{3,2,1,0:T(8,128)(2,1)} %get-tuple-element.165, s32[]{:T(128)S(6)} %select_n.26, bf16[8,32,16,256]{3,2,1,0:T(8,128)(2,1)} %get-tuple-element.164), kind=kOutput, calls=%fused_computation.clone.1 | convolution fusion | flops 875823104 | bytes 10486784 | tf_op jit(solution)/shard_map/while/body/eval_jaxpr/tgrd,gtrf->gdf/dot_general | solution.py:82
  259.3 1.0 convert_reduce_fusion.2
  260.3 2.1 select_add_fusion.2
  262.4 4.0 %bitcast_convert_fusion.2 = bf16[4,256,3328]{2,1,0:T(8,128)(2,1)S(1)} fusion(bf16[32,8,16,3328]{3,2,1,0:T(8,128)(2,1)} %get-tuple-element.165, s32[]{:T(128)S(6)} %select_n.26, bf16[8,32,16,256]{3,2,1,0:T(8,128)(2,1)} %get-tuple-element.164), kind=kOutput, calls=%fused_computation.clone.1 | convolution fusion | flops 875823104 | bytes 10486784 | tf_op jit(solution)/shard_map/while/body/eval_jaxpr/tgrd,gtrf->gdf/dot_general | solution.py:82
  266.4 1.0 convert_reduce_fusion.2
  267.4 4.1 %select_add_fusion.2 = f32[256,3328]{1,0:T(8,128)} fusion(f32[256,3328]{1,0:T(8,128)S(1)} %convert_reduce_fusion.2, f32[256,3328]{1,0:T(8,128)} %get-tuple-element.155, pred[]{:T(512)S(6)} %compare.3), kind=kLoop, calls=%fused_computation.2.clone.1 | loop fusion | flops 1703936 | bytes 10223617 | tf_op jit(solution)/shard_map/while/body/eval_jaxpr/add | solution.py:86
  271.5 4.0 %bitcast_convert_fusion.2 = bf16[4,256,3328]{2,1,0:T(8,128)(2,1)S(1)} fusion(bf16[32,8,16,3328]{3,2,1,0:T(8,128)(2,1)} %get-tuple-element.165, s32[]{:T(128)S(6)} %select_n.26, bf16[8,32,16,256]{3,2,1,0:T(8,128)(2,1)} %get-tuple-element.164), kind=kOutput, calls=%fused_computation.clone.1 | convolution fusion | flops 875823104 | bytes 10486784 | tf_op jit(solution)/shard_map/while/body/eval_jaxpr/tgrd,gtrf->gdf/dot_general | solution.py:82
  275.6 1.0 convert_reduce_fusion.2
  276.6 4.1 %select_add_fusion.2 = f32[256,3328]{1,0:T(8,128)} fusion(f32[256,3328]{1,0:T(8,128)S(1)} %convert_reduce_fusion.2, f32[256,3328]{1,0:T(8,128)} %get-tuple-element.155, pred[]{:T(512)S(6)} %compare.3), kind=kLoop, calls=%fused_computation.2.clone.1 | loop fusion | flops 1703936 | bytes 10223617 | tf_op jit(solution)/shard_map/while/body/eval_jaxpr/add | solution.py:86
  280.7 4.0 %bitcast_convert_fusion.2 = bf16[4,256,3328]{2,1,0:T(8,128)(2,1)S(1)} fusion(bf16[32,8,16,3328]{3,2,1,0:T(8,128)(2,1)} %get-tuple-element.165, s32[]{:T(128)S(6)} %select_n.26, bf16[8,32,16,256]{3,2,1,0:T(8,128)(2,1)} %get-tuple-element.164), kind=kOutput, calls=%fused_computation.clone.1 | convolution fusion | flops 875823104 | bytes 10486784 | tf_op jit(solution)/shard_map/while/body/eval_jaxpr/tgrd,gtrf->gdf/dot_general | solution.py:82
  284.7 1.0 convert_reduce_fusion.2
  285.7 4.1 %select_add_fusion.2 = f32[256,3328]{1,0:T(8,128)} fusion(f32[256,3328]{1,0:T(8,128)S(1)} %convert_reduce_fusion.2, f32[256,3328]{1,0:T(8,128)} %get-tuple-element.155, pred[]{:T(512)S(6)} %compare.3), kind=kLoop, calls=%fused_computation.2.clone.1 | loop fusion | flops 1703936 | bytes 10223617 | tf_op jit(solution)/shard_map/while/body/eval_jaxpr/add | solution.py:86
  289.8 4.0 %bitcast_convert_fusion.2 = bf16[4,256,3328]{2,1,0:T(8,128)(2,1)S(1)} fusion(bf16[32,8,16,3328]{3,2,1,0:T(8,128)(2,1)} %get-tuple-element.165, s32[]{:T(128)S(6)} %select_n.26, bf16[8,32,16,256]{3,2,1,0:T(8,128)(2,1)} %get-tuple-element.164), kind=kOutput, calls=%fused_computation.clone.1 | convolution fusion | flops 875823104 | bytes 10486784 | tf_op jit(solution)/shard_map/while/body/eval_jaxpr/tgrd,gtrf->gdf/dot_general | solution.py:82
  293.8 1.0 convert_reduce_fusion.2
  294.8 4.1 %select_add_fusion.2 = f32[256,3328]{1,0:T(8,128)} fusion(f32[256,3328]{1,0:T(8,128)S(1)} %convert_reduce_fusion.2, f32[256,3328]{1,0:T(8,128)} %get-tuple-element.155, pred[]{:T(512)S(6)} %compare.3), kind=kLoop, calls=%fused_computation.2.clone.1 | loop fusion | flops 1703936 | bytes 10223617 | tf_op jit(solution)/shard_map/while/body/eval_jaxpr/add | solution.py:86
  298.9 4.0 %bitcast_convert_fusion.2 = bf16[4,256,3328]{2,1,0:T(8,128)(2,1)S(1)} fusion(bf16[32,8,16,3328]{3,2,1,0:T(8,128)(2,1)} %get-tuple-element.165, s32[]{:T(128)S(6)} %select_n.26, bf16[8,32,16,256]{3,2,1,0:T(8,128)(2,1)} %get-tuple-element.164), kind=kOutput, calls=%fused_computation.clone.1 | convolution fusion | flops 875823104 | bytes 10486784 | tf_op jit(solution)/shard_map/while/body/eval_jaxpr/tgrd,gtrf->gdf/dot_general | solution.py:82
  302.9 1.0 convert_reduce_fusion.2
  303.9 4.1 %select_add_fusion.2 = f32[256,3328]{1,0:T(8,128)} fusion(f32[256,3328]{1,0:T(8,128)S(1)} %convert_reduce_fusion.2, f32[256,3328]{1,0:T(8,128)} %get-tuple-element.155, pred[]{:T(512)S(6)} %compare.3), kind=kLoop, calls=%fused_computation.2.clone.1 | loop fusion | flops 1703936 | bytes 10223617 | tf_op jit(solution)/shard_map/while/body/eval_jaxpr/add | solution.py:86
  308.0 4.0 %bitcast_convert_fusion.2 = bf16[4,256,3328]{2,1,0:T(8,128)(2,1)S(1)} fusion(bf16[32,8,16,3328]{3,2,1,0:T(8,128)(2,1)} %get-tuple-element.165, s32[]{:T(128)S(6)} %select_n.26, bf16[8,32,16,256]{3,2,1,0:T(8,128)(2,1)} %get-tuple-element.164), kind=kOutput, calls=%fused_computation.clone.1 | convolution fusion | flops 875823104 | bytes 10486784 | tf_op jit(solution)/shard_map/while/body/eval_jaxpr/tgrd,gtrf->gdf/dot_general | solution.py:82
  312.0 1.0 convert_reduce_fusion.2
  313.1 4.1 %select_add_fusion.2 = f32[256,3328]{1,0:T(8,128)} fusion(f32[256,3328]{1,0:T(8,128)S(1)} %convert_reduce_fusion.2, f32[256,3328]{1,0:T(8,128)} %get-tuple-element.155, pred[]{:T(512)S(6)} %compare.3), kind=kLoop, calls=%fused_computation.2.clone.1 | loop fusion | flops 1703936 | bytes 10223617 | tf_op jit(solution)/shard_map/while/body/eval_jaxpr/add | solution.py:86
  317.1 4.0 %bitcast_convert_fusion.2 = bf16[4,256,3328]{2,1,0:T(8,128)(2,1)S(1)} fusion(bf16[32,8,16,3328]{3,2,1,0:T(8,128)(2,1)} %get-tuple-element.165, s32[]{:T(128)S(6)} %select_n.26, bf16[8,32,16,256]{3,2,1,0:T(8,128)(2,1)} %get-tuple-element.164), kind=kOutput, calls=%fused_computation.clone.1 | convolution fusion | flops 875823104 | bytes 10486784 | tf_op jit(solution)/shard_map/while/body/eval_jaxpr/tgrd,gtrf->gdf/dot_general | solution.py:82
  321.2 1.0 convert_reduce_fusion.2
  322.2 4.1 %select_add_fusion.2 = f32[256,3328]{1,0:T(8,128)} fusion(f32[256,3328]{1,0:T(8,128)S(1)} %convert_reduce_fusion.2, f32[256,3328]{1,0:T(8,128)} %get-tuple-element.155, pred[]{:T(512)S(6)} %compare.3), kind=kLoop, calls=%fused_computation.2.clone.1 | loop fusion | flops 1703936 | bytes 10223617 | tf_op jit(solution)/shard_map/while/body/eval_jaxpr/add | solution.py:86
  326.3 6.5 %subtract_convert_fusion = (bf16[256,3328]{1,0:T(8,128)(2,1)S(1)}, f32[256,3328]{1,0:T(8,128)}) fusion(f32[256,3328]{1,0:T(8,128)} %param.11, f32[]{:T(128)} %bitcast.5, f32[256,3328]{1,0:T(8,128)} %get-tuple-element.81, bf16[256,3328]{1,0:T(8,128)(2,1)} %param.13, f32[]{:T(128)} %bitcast.4, bf16[256,3328]{1,0:T(8,128)(2,1)} %param.12), kind=kLoop, calls=%fused_computation.14 | loop fusion | flops 15335424 | bytes 15335432 | tf_op jit(solution)/shard_map/convert_element_type | solution.py:97
  332.8 4.0 %collective-permute-start = (bf16[256,256]{1,0:T(8,128)(2,1)S(1)}, bf16[256,256]{1,0:T(8,128)(2,1)S(1)}, u32[]{:S(2)}, u32[]{:S(2)}) collective-permute-start(bf16[256,256]{1,0:T(8,128)(2,1)S(1)} %get-tuple-element.120), channel_id=1, source_target_pairs={{0,1},{1,2},{2,3},{3,4},{4,5},{5,6},{6,7},{8,9},{9,10},{10,11},{11... | collective-permute-start | bytes 393224 | tf_op jit(solution)/shard_map/ppermute | solution.py:27
  336.8 1.9 collective-permute-start.1
  338.7 0.6 iota_compare_fusion
  339.4 0.6 dynamic_slice.25
  340.6 0.1 pad_dynamic-slice_fusion.3
  340.7 0.0 collective-permute-done
  340.7 2.4 collective-permute-done.1
  343.1 3.1 fusion.12
  (3 shorter events, 0.0 us)
Async XLA Ops:
  7.2 49.8 %all-gather.3.cloned.1.call-start = ((), (), s32[]{:S(2)}) async-start(), calls=%async_computation.1 | async-start | bytes 2359296 | tf_op jit(solution)/shard_map/all_gather | solution.py:67
  31.3 223.9 %all-gather.5.cloned.1.call-start = ((), (), s32[]{:S(2)}) async-start(), calls=%async_computation.2 | async-start | bytes 28114944 | tf_op jit(solution)/shard_map/all_gather | solution.py:73
  332.8 7.9 %collective-permute-start = (bf16[256,256]{1,0:T(8,128)(2,1)S(1)}, bf16[256,256]{1,0:T(8,128)(2,1)S(1)}, u32[]{:S(2)}, u32[]{:S(2)}) collective-permute-start(bf16[256,256]{1,0:T(8,128)(2,1)S(1)} %get-tuple-element.120), channel_id=1, source_target_pairs={{0,1},{1,2},{2,3},{3,4},{4,5},{5,6},{6,7},{8,9},{9,10},{10,11},{11... | collective-permute-start | bytes 393224 | tf_op jit(solution)/shard_map/ppermute | solution.py:27
  336.8 6.3 %collective-permute-start.1 = (bf16[256,256]{1,0:T(8,128)(2,1)S(1)}, bf16[256,256]{1,0:T(8,128)(2,1)S(1)}, u32[]{:S(2)}, u32[]{:S(2)}) collective-permute-start(bf16[256,256]{1,0:T(8,128)(2,1)S(1)} %get-tuple-element.119), channel_id=1, source_target_pairs={{1,0},{2,1},{3,2},{4,3},{5,4},{6,5},{7,6},{9,8},{10,9},{11,10},{12... | collective-permute-start | bytes 393224 | tf_op jit(solution)/shard_map/ppermute | solution.py:29
Sparse Core Ops, SparseCore 0:
  31.5 25.4 all-gather.2
  59.5 195.6 all-gather.4
where the time goes:
time: 354 us; the launch traced here: 353 us
  waiting for transfers between devices  223 us (63%)
  other arithmetic  50.5 us (14%)
  matrix products  32.1 us (9%)
  blocking collectives  23.1 us (7%)
  between operations  15.5 us (4%)
  starting transfers between devices  6.03 us (2%)
    all_gather x1, waiting for transfers between devices, per_device(): shard_piece = lax.all_gather(hidden, 'dp', axis=0, tiled=True)  198 us
    dot_general x8, matrix products, one_turn(): jnp.einsum('tgrd,gtrf->gdf', grad_block, act_block, preferred_element_typ...  32.1 us
    add x8, other arithmetic, one_turn(): return running + jnp.sum(rounded, axis=0)  30.8 us
    all_to_all x1, blocking collectives, per_device(): lax.all_to_all(out_grad, 'dp', split_axis=1, concat_axis=0, tiled=True)  23.1 us
    all_gather x1, waiting for transfers between devices, per_device(): spread = lax.all_gather(regrouped, 'tensor', axis=0, tiled=True)  21.4 us
    reduce_sum x8, other arithmetic, one_turn(): return running + jnp.sum(rounded, axis=0)  7.96 us
  transfers between devices with their start and end apart: 4, of which 3 were waited for; matrix products, arithmetic and copies ran while one was open for 1% of the time, Pallas kernels for 0%

commit v1 on v0

v1 whole, which is shorter than its diff:
```python
import jax
import jax.numpy as jnp
import numpy as np
from jax import lax
from jax.sharding import Mesh, PartitionSpec as P

DRIFT = 256
CAP = 3840
CHUNKS = ((0, 896), (2432, 3328), (896, 1664), (1664, 2432))

beta_first = 0.9
beta_second = 0.95
epsilon = 1e-08
decay_rate = 0.1
learn_rate = 0.001

TENSOR = ("x", "core")


def adamw(gradient, master, first_moment, second_moment, first_fix, second_fix):
    first_new = beta_first * first_moment + (1.0 - beta_first) * gradient
    second_new = beta_second * second_moment + (1.0 - beta_second) * gradient * gradient
    update = (
        first_new / first_fix / (jnp.sqrt(second_new / second_fix) + epsilon) + decay_rate * master
    )
    master_new = master - learn_rate * update
    return (master_new, update)


def per_device(hidden, out_grad, master, first_moment, second_moment, row_counts, step_count):
    width = hidden.shape[1]
    tensor_count = lax.axis_size(TENSOR)
    z_count = lax.axis_size("z")
    local_tokens = out_grad.shape[0]
    features = out_grad.shape[1] // z_count

    regrouped = lax.all_to_all(out_grad, "z", split_axis=1, concat_axis=0, tiled=True)
    spread = lax.all_gather(regrouped, TENSOR, axis=0, tiled=True)
    cotangent = spread.reshape(tensor_count, z_count, local_tokens, features)
    cotangent = cotangent.transpose(1, 0, 2, 3).reshape(-1, features)

    steps_done = step_count[0].astype(jnp.float32)
    first_fix = 1.0 - jnp.power(beta_first, steps_done)
    second_fix = 1.0 - jnp.power(beta_second, steps_done)

    gathered = [
        lax.all_gather(hidden[:, low:high], "z", axis=0, tiled=True) for low, high in CHUNKS
    ]
    updates = {}
    weights = {}
    for (low, high), acts in zip(CHUNKS, gathered):
        partial_value = lax.dot_general(
            cotangent, acts, (((0,), (0,)), ((), ())), preferred_element_type=jnp.float32
        ).astype(jnp.bfloat16)
        gradient = lax.psum_scatter(partial_value, "y", scatter_dimension=0, tiled=True)
        master_new, update = adamw(
            gradient.astype(jnp.float32),
            master[:, low:high],
            first_moment[:, low:high].astype(jnp.float32),
            second_moment[:, low:high].astype(jnp.float32),
            first_fix,
            second_fix,
        )
        updates[low] = update
        weights[low] = master_new.astype(jnp.bfloat16)

    order = sorted(updates)
    head = weights[order[0]][:, :DRIFT]
    tail = weights[order[-1]][:, -DRIFT:]
    ends = tensor_count - 1
    left = lax.ppermute(tail, TENSOR, [(i, i + 1) for i in range(ends)])
    right = lax.ppermute(head, TENSOR, [(i + 1, i) for i in range(ends)])

    position = lax.axis_index(TENSOR)
    places = jnp.arange(tensor_count, dtype=jnp.int32)
    first_slot = jnp.sum(jnp.where(places < position, row_counts, 0))
    length = jnp.sum(jnp.where(places == position, row_counts, 0))
    rows = master.shape[0]
    widened = jnp.concatenate(
        [left] + [weights[k] for k in order] + [right, jnp.zeros((rows, 2 * DRIFT), jnp.bfloat16)],
        axis=1,
    )
    start = first_slot - position * width + DRIFT
    window = lax.dynamic_slice_in_dim(widened, start, CAP, 1)
    slot_index = jnp.arange(CAP, dtype=jnp.int32)
    laid = jnp.where((slot_index < length)[None, :], window, jnp.zeros((), jnp.bfloat16))
    return (jnp.concatenate([updates[k] for k in order], axis=1), laid)


def solution(mesh):
    fine = Mesh(np.asarray(mesh.devices).reshape(8, 4, 4, 2), ("z", "y", "x", "core"))
    dp = ("z", "y")
    return jax.shard_map(
        per_device,
        mesh=fine,
        in_specs=(
            P(dp, TENSOR),
            P(dp + TENSOR, None),
            P(dp, TENSOR),
            P(dp, TENSOR),
            P(dp, TENSOR),
            P(),
            P(),
        ),
        out_specs=(P(dp, TENSOR), P(dp, TENSOR)),
        check_vma=False,
    )
```

time: 354 us -> 359 us (1.014)
  waiting for transfers between devices: 223 us -> 273 us
  other arithmetic: 50.5 us -> 17.1 us
  matrix products: 32.1 us -> 19.1 us
  local copies, waits for them, and re-layouts: 2.92 us -> 7.89 us
  blocking collectives: 23.1 us -> 19.3 us
    reduce_scatter x0 -> x4, waiting for transfers between devices: none -> 106 us  [per_device(): lax.psum_scatter(partial_value, 'y', scatter_dimension=0, tiled=True)]
    all_gather x2 -> x5, waiting for transfers between devices: 220 us -> 166 us  [the longest x4 144 us: per_device(): lax.all_gather(hidden[:, low:high], 'z', axis=0, tiled=True)]
    add x8 -> x0, other arithmetic: 30.8 us -> none  [one_turn(): return running + jnp.sum(rounded, axis=0)]
    dot_general x8 -> x4, matrix products: 32.1 us -> 19.1 us  [per_device(): lax.dot_general(cotangent, acts, (((0,), (0,)), ((), ())), preferred_elem...]
    unnamed x1 -> x3, other arithmetic: 0.01 us -> 9.14 us
    reduce_sum x8 -> x1, other arithmetic: 7.96 us -> 0.64 us  [per_device(): length = jnp.sum(jnp.where(places == position, row_counts, 0))]
    convert_element_type x1, other arithmetic: 6.5 us -> 2.37 us  [per_device(): weights[low] = master_new.astype(jnp.bfloat16)]
    all_to_all x1, blocking collectives: 23.1 us -> 19.3 us  [per_device(): lax.all_to_all(out_grad, 'z', split_axis=1, concat_axis=0, tiled=True)]
  transfers between devices with their start and end apart: 4 -> 11, of which waited for: 3 -> 9; matrix products, arithmetic and copies ran while one was open for 1% -> 11% of each run, Pallas kernels for 0% -> 0%
where the time goes in v1:
time: 359 us; the launch traced here: 358 us
  waiting for transfers between devices  273 us (76%)
  blocking collectives  19.3 us (5%)
  matrix products  19.1 us (5%)
  other arithmetic  17.1 us (5%)
  between operations  15.3 us (4%)
  local copies, waits for them, and re-layouts  7.89 us (2%)
  starting transfers between devices  6.69 us (2%)
    all_gather x4, waiting for transfers between devices, per_device(): lax.all_gather(hidden[:, low:high], 'z', axis=0, tiled=True)  144 us
    reduce_scatter x4, waiting for transfers between devices, per_device(): lax.psum_scatter(partial_value, 'y', scatter_dimension=0, tiled=True)  106 us
    all_gather x1, waiting for transfers between devices, per_device(): spread = lax.all_gather(regrouped, TENSOR, axis=0, tiled=True)  21.2 us
    all_to_all x1, blocking collectives, per_device(): lax.all_to_all(out_grad, 'z', split_axis=1, concat_axis=0, tiled=True)  19.3 us
    dot_general x4, matrix products, per_device(): lax.dot_general(cotangent, acts, (((0,), (0,)), ((), ())), preferred_elem...  19.1 us
    unnamed x3, other arithmetic  9.14 us
  transfers between devices with their start and end apart: 11, of which 9 were waited for; matrix products, arithmetic and copies ran while one was open for 11% of the time, Pallas kernels for 0%

profile of v1, /device:TPU:1, one launch (start us, length us, event | category | flops | bytes accessed | tf_op | source)
XLA Modules:
  0.0 358.4 jit_solution(4531047940108893145)
XLA Ops:
  7.2 0.0 all-gather.6.cloned.1.call-start
  7.2 1.0 copy.16
  8.2 19.3 %all_to_all.19 = bf16[16,8,1024]{2,0,1:T(8,128)(2,1)} all-to-all(bf16[16,8,1024]{2,0,1:T(8,128)(2,1)S(1)} %bitcast.27), channel_id=1, replica_groups=mesh['z'=8,'y'=4,'x'=4,'core'=2] {'z'}, dimensions={1} | all-to-all | bytes 524288 | tf_op jit(solution)/shard_map/all_to_all | solution.py:37
  27.5 0.0 all-gather.6.cloned.1.call-update
  27.5 0.0 all-gather.14.cloned.1.call-start
  27.5 1.9 fusion.41
  29.4 0.0 all-gather.14.cloned.1.call-update
  29.4 0.0 all-gather.8.cloned.1.call-start
  29.5 0.7 all-gather.8.cloned.1.call-update
  30.2 0.0 all-gather.10.cloned.1.call-start
  30.2 1.8 fusion.40
  32.0 0.0 all-gather.10.cloned.1.call-update
  32.0 0.0 all-gather.12.cloned.1.call-start
  32.1 0.5 all-gather.12.cloned.1.call-update
  32.6 0.0 reduce-scatter.11.cloned.1.call-start
  32.7 21.2 %all-gather.6.cloned.1.call-done = bf16[1024,1024]{1,0:T(8,128)(2,1)} async-done(((bf16[128,1024]{1,0:T(8,128)(2,1)}), bf16[1024,1024]{1,0:T(8,128)(2,1)}) %all-gather.6.cloned.1.call-update) | async-done | bytes 2097168 | tf_op jit(solution)/shard_map/all_gather | solution.py:38
  53.9 1.8 copy.13
  55.7 37.4 %all-gather.14.cloned.1.call-done = bf16[1024,896]{1,0:T(8,128)(2,1)} async-done(((bf16[128,896]{1,0:T(8,128)(2,1)}), bf16[1024,896]{1,0:T(8,128)(2,1)}) %all-gather.14.cloned.1.call-update) | async-done | bytes 1835024 | tf_op jit(solution)/shard_map/all_gather | solution.py:47
  93.1 5.1 %convolution_convert_fusion = bf16[1024,896]{1,0:T(8,128)(2,1)} fusion(bf16[1024,1024]{1,0:T(8,128)(2,1)S(1)} %bitcast.22, bf16[1024,896]{1,0:T(8,128)(2,1)} %all-gather.14.cloned.1.call-done), kind=kOutput, calls=%fused_computation.2 | convolution fusion | flops 1879965696 | bytes 5767168 | tf_op jit(solution)/shard_map/dot_general | solution.py:52
  98.2 0.0 reduce-scatter.11.cloned.1.call-update
  98.2 0.0 reduce-scatter.5.cloned.1.call-start
  98.3 36.4 %all-gather.8.cloned.1.call-done = bf16[1024,896]{1,0:T(8,128)(2,1)} async-done(((bf16[128,896]{1,0:T(8,128)(2,1)}), bf16[1024,896]{1,0:T(8,128)(2,1)}) %all-gather.8.cloned.1.call-update) | async-done | bytes 1835024 | tf_op jit(solution)/shard_map/all_gather | solution.py:47
  134.7 5.1 %convolution_convert_fusion.1 = bf16[1024,896]{1,0:T(8,128)(2,1)} fusion(bf16[1024,1024]{1,0:T(8,128)(2,1)S(1)} %bitcast.23, bf16[1024,896]{1,0:T(8,128)(2,1)} %all-gather.8.cloned.1.call-done), kind=kOutput, calls=%fused_computation.3 | convolution fusion | flops 1879965696 | bytes 5767168 | tf_op jit(solution)/shard_map/dot_general | solution.py:52
  139.8 0.0 reduce-scatter.5.cloned.1.call-update
  139.8 0.0 reduce-scatter.7.cloned.1.call-start
  139.8 34.9 %all-gather.10.cloned.1.call-done = bf16[1024,768]{1,0:T(8,128)(2,1)} async-done(((bf16[128,768]{1,0:T(8,128)(2,1)}), bf16[1024,768]{1,0:T(8,128)(2,1)}) %all-gather.10.cloned.1.call-update) | async-done | bytes 1572880 | tf_op jit(solution)/shard_map/all_gather | solution.py:47
  174.8 4.4 %convolution_convert_fusion.3 = bf16[1024,768]{1,0:T(8,128)(2,1)} fusion(bf16[1024,1024]{1,0:T(8,128)(2,1)S(1)} %bitcast.24, bf16[1024,768]{1,0:T(8,128)(2,1)} %all-gather.10.cloned.1.call-done), kind=kOutput, calls=%fused_computation.5 | convolution fusion | flops 1611399168 | bytes 5242880 | tf_op jit(solution)/shard_map/dot_general | solution.py:52
  179.2 0.0 reduce-scatter.7.cloned.1.call-update
  179.2 0.0 reduce-scatter.9.cloned.1.call-start
  179.3 35.8 %all-gather.12.cloned.1.call-done = bf16[1024,768]{1,0:T(8,128)(2,1)} async-done(((bf16[128,768]{1,0:T(8,128)(2,1)}), bf16[1024,768]{1,0:T(8,128)(2,1)}) %all-gather.12.cloned.1.call-update) | async-done | bytes 1572880 | tf_op jit(solution)/shard_map/all_gather | solution.py:47
  215.0 4.4 %convolution_convert_fusion.2 = bf16[1024,768]{1,0:T(8,128)(2,1)} fusion(bf16[1024,1024]{1,0:T(8,128)(2,1)S(1)} %bitcast.25, bf16[1024,768]{1,0:T(8,128)(2,1)} %all-gather.12.cloned.1.call-done), kind=kOutput, calls=%fused_computation.4 | convolution fusion | flops 1611399168 | bytes 5242880 | tf_op jit(solution)/shard_map/dot_general | solution.py:52
  220.2 30.4 %reduce-scatter.11.cloned.1.call-done = bf16[256,896]{1,0:T(8,128)(2,1)} async-done(((bf16[1024,896]{1,0:T(8,128)(2,1)}), bf16[256,896]{1,0:T(8,128)(2,1)}) %reduce-scatter.11.cloned.1.call-update) | async-done | bytes 458768 | tf_op jit(solution)/shard_map/reduce_scatter | solution.py:55
  250.7 2.4 subtract_convert_fusion.1
  253.1 3.6 %collective-permute-start = (bf16[256,256]{1,0:T(8,128)(2,1)S(1)}, bf16[256,256]{1,0:T(8,128)(2,1)S(1)}, u32[]{:S(2)}, u32[]{:S(2)}) collective-permute-start(bf16[256,256]{1,0:T(8,128)(2,1)S(1)} %slice.72), channel_id=1, source_target_pairs={{0,1},{1,2},{2,3},{3,4},{4,5},{5,6},{6,7},{8,9},{9,10},{10,11},{11... | collective-permute-start | bytes 393224 | tf_op jit(solution)/shard_map/ppermute | solution.py:71
  256.7 0.6 fusion.34
  257.9 0.7 iota_compare_fusion
  258.5 0.0 collective-permute-done
  258.6 0.7 constant_dynamic-update-slice_fusion.3
  259.3 24.4 %reduce-scatter.5.cloned.1.call-done = bf16[256,896]{1,0:T(8,128)(2,1)} async-done(((bf16[1024,896]{1,0:T(8,128)(2,1)}), bf16[256,896]{1,0:T(8,128)(2,1)}) %reduce-scatter.5.cloned.1.call-update) | async-done | bytes 458768 | tf_op jit(solution)/shard_map/reduce_scatter | solution.py:55
  283.7 3.2 constant_dynamic-update-slice_fusion.2
  286.9 2.7 collective-permute-start.1
  289.7 23.6 %reduce-scatter.7.cloned.1.call-done = bf16[256,768]{1,0:T(8,128)(2,1)} async-done(((bf16[1024,768]{1,0:T(8,128)(2,1)}), bf16[256,768]{1,0:T(8,128)(2,1)}) %reduce-scatter.7.cloned.1.call-update) | async-done | bytes 393232 | tf_op jit(solution)/shard_map/reduce_scatter | solution.py:55
  313.2 3.0 fusion.32
  316.2 27.6 %reduce-scatter.9.cloned.1.call-done = bf16[256,768]{1,0:T(8,128)(2,1)} async-done(((bf16[1024,768]{1,0:T(8,128)(2,1)}), bf16[256,768]{1,0:T(8,128)(2,1)}) %reduce-scatter.9.cloned.1.call-update) | async-done | bytes 393232 | tf_op jit(solution)/shard_map/reduce_scatter | solution.py:55
  343.8 2.9 fusion.33
  346.7 2.0 pad_maximum_fusion
  348.7 0.7 copy-done
  349.5 2.4 dynamic-slice_select_fusion
  (10 shorter events, 0.1 us)
Async XLA Ops:
  7.2 46.7 %all-gather.6.cloned.1.call-start = ((), (), s32[]{:S(2)}) async-start(), calls=%async_computation.5 | async-start | bytes 2359296 | tf_op jit(solution)/shard_map/all_gather | solution.py:38
  27.5 65.6 %all-gather.14.cloned.1.call-start = ((), (), s32[]{:S(2)}) async-start(), calls=%async_computation.12 | async-start | bytes 2064384 | tf_op jit(solution)/shard_map/all_gather | solution.py:47
  29.4 105.2 %all-gather.8.cloned.1.call-start = ((), (), s32[]{:S(2)}) async-start(), calls=%async_computation.6 | async-start | bytes 2064384 | tf_op jit(solution)/shard_map/all_gather | solution.py:47
  30.2 144.6 %all-gather.10.cloned.1.call-start = ((), (), s32[]{:S(2)}) async-start(), calls=%async_computation.8 | async-start | bytes 1769472 | tf_op jit(solution)/shard_map/all_gather | solution.py:47
  32.0 183.0 %all-gather.12.cloned.1.call-start = ((), (), s32[]{:S(2)}) async-start(), calls=%async_computation.10 | async-start | bytes 1769472 | tf_op jit(solution)/shard_map/all_gather | solution.py:47
  32.6 218.0 %reduce-scatter.11.cloned.1.call-start = ((), (), s32[]{:S(2)}) async-start(), calls=%async_computation.13 | async-start | bytes 2293760 | tf_op jit(solution)/shard_map/reduce_scatter | solution.py:55
  98.2 185.5 %reduce-scatter.5.cloned.1.call-start = ((), (), s32[]{:S(2)}) async-start(), calls=%async_computation.7 | async-start | bytes 2293760 | tf_op jit(solution)/shard_map/reduce_scatter | solution.py:55
  139.8 173.4 %reduce-scatter.7.cloned.1.call-start = ((), (), s32[]{:S(2)}) async-start(), calls=%async_computation.9 | async-start | bytes 1966080 | tf_op jit(solution)/shard_map/reduce_scatter | solution.py:55
  179.2 164.6 %reduce-scatter.9.cloned.1.call-start = ((), (), s32[]{:S(2)}) async-start(), calls=%async_computation.11 | async-start | bytes 1966080 | tf_op jit(solution)/shard_map/reduce_scatter | solution.py:55
  219.5 37.2 %copy-start.1 = (s32[8]{0:T(128)S(1)}, s32[8]{0:T(128)}, u32[]{:S(2)}) copy-start(s32[8]{0:T(128)} %param.12) | copy-start | bytes 100
  253.1 5.5 %collective-permute-start = (bf16[256,256]{1,0:T(8,128)(2,1)S(1)}, bf16[256,256]{1,0:T(8,128)(2,1)S(1)}, u32[]{:S(2)}, u32[]{:S(2)}) collective-permute-start(bf16[256,256]{1,0:T(8,128)(2,1)S(1)} %slice.72), channel_id=1, source_target_pairs={{0,1},{1,2},{2,3},{3,4},{4,5},{5,6},{6,7},{8,9},{9,10},{10,11},{11... | collective-permute-start | bytes 393224 | tf_op jit(solution)/shard_map/ppermute | solution.py:71
  286.9 62.6 %collective-permute-start.1 = (bf16[256,256]{1,0:T(8,128)(2,1)S(1)}, bf16[256,256]{1,0:T(8,128)(2,1)S(1)}, u32[]{:S(2)}, u32[]{:S(2)}) collective-permute-start(bf16[256,256]{1,0:T(8,128)(2,1)S(1)} %slice.73), channel_id=1, source_target_pairs={{1,0},{2,1},{3,2},{4,3},{5,4},{6,5},{7,6},{9,8},{10,9},{11,10},{12... | collective-permute-start | bytes 393224 | tf_op jit(solution)/shard_map/ppermute | solution.py:72
  346.7 2.7 copy-start
Sparse Core Ops, SparseCore 0:
  27.6 26.2 all-gather.5
  56.2 36.7 all-gather.13
  95.5 39.1 all-gather.7
  136.3 38.4 all-gather.9
  176.4 38.5 all-gather.11
  218.0 32.5 reduce-scatter.10
  253.8 29.8 reduce-scatter.4
  286.2 26.9 reduce-scatter.6
  315.8 27.9 reduce-scatter.8

commit v2 on v1

v2 whole, which is shorter than its diff:
```python
import functools

import jax
import jax.numpy as jnp
import numpy as np
from jax import lax
from jax.experimental import pallas as pl
from jax.experimental.pallas import tpu as pltpu
from jax.sharding import Mesh, PartitionSpec as P

DRIFT = 256
CAP = 3840
N_Z = 8
N_Y = 4
N_X = 4
LEFT = 640
RIGHT = 2688

beta_first = 0.9
beta_second = 0.95
epsilon = 1e-08
decay_rate = 0.1
learn_rate = 0.001

TENSOR = ("x", "core")


def shift(value, axis, count, by):
    return lax.ppermute(value, axis, [(i, (i + by) % count) for i in range(count)])


def both_ways(up, down):
    return shift(up, "z", N_Z, 1), shift(down, "z", N_Z, -1)


def ring_gather(block, first, farther):
    up, down = first
    pieces = [(block, 0), (up, -1), (down, 1)]
    for step in range(2, N_Z // 2):
        up, down = both_ways(up, down)
        pieces += [(up, -step), (down, step)]
    last = shift(up if farther > 0 else down, "z", N_Z, farther)
    return pieces + [(last, N_Z // 2)]


def cotangent_of(mine, tokens):
    rows, features = mine.shape
    count = 2 * N_X
    y = lax.axis_index("y")
    copies = jnp.broadcast_to(mine[None], (count, rows, features))
    spread = lax.all_to_all(copies, TENSOR, split_axis=0, concat_axis=0, tiled=True)
    spread = spread.reshape(count, N_Z, tokens, features).transpose(1, 0, 2, 3)
    spread = spread.reshape(-1, features)
    size = features // N_Y
    cut = size // 2

    def taken(by, start):
        return lax.dynamic_slice_in_dim(spread, ((y + by) % N_Y) * size + start, cut, 1)

    order = ((2, 0), (1, cut), (2, cut), (3, 0), (1, 0), (3, cut), (0, 0), (0, cut))
    return jnp.concatenate([taken(*k) for k in order], axis=1)


def partials_body(offsets, z_ref, cot_ref, *refs):
    pieces = refs[: len(offsets)]
    outs = refs[len(offsets) : -1]
    acts_ref = refs[-1]
    z = z_ref[0]
    for piece, offset in zip(pieces, offsets):
        rows = piece.shape[0]
        group = lax.rem(z + (offset + N_Z), N_Z)
        acts_ref[pl.ds(pl.multiple_of(group * rows, rows), rows), :] = piece[...]
    low = 0
    for out in outs:
        size = out.shape[0]
        out[...] = lax.dot_general(
            cot_ref[:, low : low + size],
            acts_ref[...],
            (((0,), (0,)), ((), ())),
            preferred_element_type=jnp.float32,
        ).astype(out.dtype)
        low += size


def partials(z, cotangent, pieces, low, cols, tile):
    tokens, features = cotangent.shape
    rows = features // N_Y
    first = low // tile
    along = lambda i: (0, i)
    shifted = lambda i: (0, i + first)
    sizes = (rows, rows, rows, rows)
    kinds = (jnp.bfloat16, jnp.bfloat16, jnp.bfloat16, jnp.float32)
    body = functools.partial(partials_body, tuple(p[1] for p in pieces))
    return pl.pallas_call(
        body,
        grid=(cols // tile,),
        in_specs=[
            pl.BlockSpec(memory_space=pltpu.SMEM),
            pl.BlockSpec(cotangent.shape, lambda i: (0, 0)),
        ]
        + [pl.BlockSpec((p[0].shape[0], tile), shifted) for p in pieces],
        out_specs=[pl.BlockSpec((size, tile), along) for size in sizes],
        out_shape=[
            jax.ShapeDtypeStruct((size, cols), kind) for size, kind in zip(sizes, kinds)
        ],
        scratch_shapes=[pltpu.VMEM((tokens, tile), jnp.bfloat16)],
        compiler_params=pltpu.CompilerParams(vmem_limit_bytes=20 * 1024 * 1024),
        name="partials",
    )(z, cotangent, *[pltpu.with_memory_space_constraint(p[0], pltpu.HBM) for p in pieces])


def ring_scatter(part):
    up, down, near, own = part
    half = near.shape[0] // 2
    wide = jnp.float32
    below = shift(up, "y", N_Y, 1)
    above = shift(down, "y", N_Y, -1)
    on_up = (near[:half].astype(wide) + below[:half].astype(wide)).astype(jnp.bfloat16)
    on_down = (near[half:].astype(wide) + above[:half].astype(wide)).astype(jnp.bfloat16)
    far_up = shift(on_up, "y", N_Y, 1)
    far_down = shift(on_down, "y", N_Y, -1)
    direct = jnp.concatenate([above[half:], below[half:]], axis=0).astype(wide)
    through = jnp.concatenate([far_up, far_down], axis=0).astype(wide)
    return own + direct + through


def adamw(gradient, master, first_moment, second_moment, first_fix, second_fix):
    first_new = beta_first * first_moment + (1.0 - beta_first) * gradient
    second_new = beta_second * second_moment + (1.0 - beta_second) * gradient * gradient
    update = (
        first_new / first_fix / (jnp.sqrt(second_new / second_fix) + epsilon) + decay_rate * master
    )
    master_new = master - learn_rate * update
    return (master_new, update)


def per_device(hidden, out_grad, master, first_moment, second_moment, row_counts, step_count):
    width = hidden.shape[1]
    rows = master.shape[0]
    tensor_count = lax.axis_size(TENSOR)
    z = lax.axis_index("z").astype(jnp.int32).reshape(1)

    inner = hidden[:, LEFT:RIGHT]
    rim = jnp.concatenate([hidden[:, :LEFT], hidden[:, RIGHT:]], axis=1)
    rim_near = both_ways(rim, rim)
    inner_near = both_ways(inner, inner)
    mine = lax.all_to_all(out_grad, "z", split_axis=1, concat_axis=0, tiled=True)
    rim_pieces = ring_gather(rim, rim_near, 1)
    inner_pieces = ring_gather(inner, inner_near, -1)
    _, _, mine = lax.optimization_barrier((rim_near, inner_near, mine))
    cotangent = cotangent_of(mine, out_grad.shape[0])

    steps_done = step_count[0].astype(jnp.float32)
    first_fix = 1.0 - jnp.power(beta_first, steps_done)
    second_fix = 1.0 - jnp.power(beta_second, steps_done)

    rim_gradient = ring_scatter(
        partials(z, cotangent, rim_pieces, 0, rim.shape[1], rim.shape[1] // 2)
    )
    span = (RIGHT - LEFT) // 2
    first_gradient = ring_scatter(partials(z, cotangent, inner_pieces, 0, span, span // 2))
    second_gradient = ring_scatter(partials(z, cotangent, inner_pieces, span, span, span // 2))

    updates = {}
    weights = {}
    for low, high, gradient in (
        (0, LEFT, rim_gradient[:, :LEFT]),
        (RIGHT, width, rim_gradient[:, LEFT:]),
        (LEFT, LEFT + span, first_gradient),
        (LEFT + span, RIGHT, second_gradient),
    ):
        master_new, updates[low] = adamw(
            gradient,
            master[:, low:high],
            first_moment[:, low:high].astype(jnp.float32),
            second_moment[:, low:high].astype(jnp.float32),
            first_fix,
            second_fix,
        )
        weights[low] = master_new.astype(jnp.bfloat16)
    head = weights[0][:, :DRIFT]
    tail = weights[RIGHT][:, -DRIFT:]
    last = tensor_count - 1
    left = lax.ppermute(tail, TENSOR, [(i, i + 1) for i in range(last)])
    right = lax.ppermute(head, TENSOR, [(i + 1, i) for i in range(last)])
    blank = jnp.zeros((rows, 2 * DRIFT), jnp.bfloat16)
    order = sorted(weights)
    widened = jnp.concatenate(
        [left] + [weights[k] for k in order] + [right, blank], axis=1
    )
    update = jnp.concatenate([updates[k] for k in order], axis=1)

    position = lax.axis_index(TENSOR)
    places = jnp.arange(tensor_count, dtype=jnp.int32)
    first_slot = jnp.sum(jnp.where(places < position, row_counts, 0))
    length = jnp.sum(jnp.where(places == position, row_counts, 0))
    start = first_slot - position * width + DRIFT
    window = lax.dynamic_slice_in_dim(widened, start, CAP, 1)
    slot_index = jnp.arange(CAP, dtype=jnp.int32)
    laid = jnp.where((slot_index < length)[None, :], window, jnp.zeros((), jnp.bfloat16))
    return (update, laid)


def solution(mesh):
    fine = Mesh(np.asarray(mesh.devices).reshape(N_Z, N_Y, N_X, 2), ("z", "y", "x", "core"))
    dp = ("z", "y")
    return jax.shard_map(
        per_device,
        mesh=fine,
        in_specs=(
            P(dp, TENSOR),
            P(dp + TENSOR, None),
            P(dp, TENSOR),
            P(dp, TENSOR),
            P(dp, TENSOR),
            P(),
            P(),
        ),
        out_specs=(P(dp, TENSOR), P(dp, TENSOR)),
        check_vma=False,
    )
```

time: 359 us -> 157 us (0.44)
  waiting for transfers between devices: 273 us -> 52.3 us
  starting transfers between devices: 6.69 us -> 66.9 us
  blocking collectives: 19.3 us -> 0 us
  matrix products: 19.1 us -> 0 us
  Pallas kernels: 0 us -> 13.9 us
  between operations: 15.3 us -> 2.57 us
  other arithmetic: 17.1 us -> 10.8 us
    all_gather x5 -> x0, waiting for transfers between devices: 166 us -> none  [the longest x4 144 us: per_device(): lax.all_gather(hidden[:, low:high], 'z', axis=0, tiled=True)]
    reduce_scatter x4 -> x0, waiting for transfers between devices: 106 us -> none  [per_device(): lax.psum_scatter(partial_value, 'y', scatter_dimension=0, tiled=True)]
    ppermute x2 -> x28, waiting for transfers between devices: 0.05 us -> 52.3 us  [the longest x26 52.3 us: shift(): lax.ppermute(value, axis, [(i, (i + by) % count) for i in range(count)])]
    ppermute x2 -> x28, starting transfers between devices: 6.32 us -> 56.2 us  [the longest x26 34.9 us: shift(): lax.ppermute(value, axis, [(i, (i + by) % count) for i in range(count)])]
    all_to_all x1 -> x0, blocking collectives: 19.3 us -> none  [per_device(): lax.all_to_all(out_grad, 'z', split_axis=1, concat_axis=0, tiled=True)]
    dot_general x4 -> x0, matrix products: 19.1 us -> none  [per_device(): lax.dot_general(cotangent, acts, (((0,), (0,)), ((), ())), preferred_elem...]
    pallas_call x0 -> x3, Pallas kernels: none -> 13.9 us  [partials(): pl.pallas_call(body, grid=(cols // tile,), in_specs=[pl.BlockSpec(memory_...]
    all_to_all x0 -> x2, starting transfers between devices: none -> 10.7 us  [the longest x1 5.52 us: cotangent_of(): lax.all_to_all(copies, TENSOR, split_axis=0, concat_axis=0, tiled=True)]
  transfers between devices with their start and end apart: 11 -> 30, of which waited for: 9 -> 8; matrix products, arithmetic and copies ran while one was open for 11% -> 9% of each run, Pallas kernels for 0% -> 9%
where the time goes in v2:
time: 157 us; the launch traced here: 156 us
  starting transfers between devices  66.9 us (43%)
  waiting for transfers between devices  52.3 us (33%)
  Pallas kernels  13.9 us (9%)
  other arithmetic  10.8 us (7%)
  local copies, waits for them, and re-layouts  9.95 us (6%)
  between operations  2.57 us (2%)
    ppermute x26, waiting for transfers between devices, shift(): lax.ppermute(value, axis, [(i, (i + by) % count) for i in range(count)])  52.3 us
    ppermute x26, starting transfers between devices, shift(): lax.ppermute(value, axis, [(i, (i + by) % count) for i in range(count)])  34.9 us
    pallas_call x3, Pallas kernels, partials(): pl.pallas_call(body, grid=(cols // tile,), in_specs=[pl.BlockSpec(memory_...  13.9 us
    ppermute x1, starting transfers between devices, per_device(): left = lax.ppermute(tail, TENSOR, [(i, i + 1) for i in range(last)])  11 us
    ppermute x1, starting transfers between devices, per_device(): right = lax.ppermute(head, TENSOR, [(i + 1, i) for i in range(last)])  10.4 us
    all_to_all x1, starting transfers between devices, cotangent_of(): lax.all_to_all(copies, TENSOR, split_axis=0, concat_axis=0, tiled=True)  5.52 us
    all_to_all x1, starting transfers between devices, per_device(): lax.all_to_all(out_grad, 'z', split_axis=1, concat_axis=0, tiled=True)  5.2 us
  transfers between devices with their start and end apart: 30, of which 8 were waited for; matrix products, arithmetic and copies ran while one was open for 9% of the time, Pallas kernels for 9%

profile of v2, /device:TPU:1, one launch (start us, length us, event | category | flops | bytes accessed | tf_op | source)
XLA Modules:
  0.0 156.5 jit_solution(11813275375153267205)
XLA Ops:
  0.6 1.1 slice.114.refs_0_
  1.7 2.5 %collective-permute-start.2 = (bf16[128,2048]{1,0:T(8,128)(2,1)S(1)}, bf16[128,2048]{1,0:T(8,128)(2,1)}, u32[]{:S(2)}, u32[]{:S(2)}) collective-permute-start(bf16[128,2048]{1,0:T(8,128)(2,1)S(1)} %slice.114.refs_0_), channel_id=1, source_target_pairs={{0,32},{32,64},{64,96},{96,128},{128,160},{160,192},{192,224},{224... | collective-permute-start | bytes 1572872 | tf_op jit(solution)/shard_map/ppermute | solution.py:29
  4.3 4.0 %collective-permute-start.3 = (bf16[128,2048]{1,0:T(8,128)(2,1)S(1)}, bf16[128,2048]{1,0:T(8,128)(2,1)S(1)}, u32[]{:S(2)}, u32[]{:S(2)}) collective-permute-start(bf16[128,2048]{1,0:T(8,128)(2,1)S(1)} %slice.114.refs_0_), channel_id=1, source_target_pairs={{0,224},{32,0},{64,32},{96,64},{128,96},{160,128},{192,160},{224,1... | collective-permute-start | bytes 1572872 | tf_op jit(solution)/shard_map/ppermute | solution.py:29
  8.3 1.7 %copy.16 = bf16[2,8,8,1024]{3,2,0,1:T(8,128)(2,1)} copy(bf16[2,8,8,1024]{3,2,1,0:T(8,128)(2,1)} %bitcast.24) | data formatting | bytes 524288 | tf_op jit(solution)/shard_map/all_to_all | solution.py:147
  10.0 5.2 %all-to-all-start = ((bf16[16,8,1024]{2,0,1:T(8,128)(2,1)}), bf16[16,8,1024]{2,0,1:T(8,128)(2,1)S(1)}, u32[]{:S(2)}, u32[]{:S(2)}) async-start(bf16[16,8,1024]{2,0,1:T(8,128)(2,1)} %bitcast.13), calls=%async_computation | async-start | bytes 524288 | tf_op jit(solution)/shard_map/all_to_all | solution.py:147
  15.2 1.0 fusion.28
  16.2 1.5 collective-permute-start
  17.8 1.3 collective-permute-start.1
  19.1 13.4 %collective-permute-done.refs_1_ = bf16[128,1280]{1,0:T(8,128)(2,1)S(1)} collective-permute-done((bf16[128,1280]{1,0:T(8,128)(2,1)S(1)}, bf16[128,1280]{1,0:T(8,128)(2,1)S(1)}, u32[]{:S(2)}, u32[]{:S(2)}) %collective-permute-start) | collective-permute-done | bytes 327712 | tf_op jit(solution)/shard_map/ppermute | solution.py:29
  32.5 1.7 %broadcast_in_dim.27 = bf16[8,128,1024]{2,1,0:T(8,128)(2,1)} broadcast(bf16[128,1024]{1,0:T(8,128)(2,1)S(1)} %bitcast.23), dimensions={1,2} | broadcast | bytes 2359296 | tf_op jit(solution)/shard_map/broadcast_in_dim | solution.py:50
  34.2 5.5 %all-to-all-start.1 = ((bf16[8,128,1024]{2,1,0:T(8,128)(2,1)}), bf16[8,128,1024]{2,1,0:T(8,128)(2,1)S(1)}, u32[]{:S(2)}, u32[]{:S(2)}) async-start(bf16[8,128,1024]{2,1,0:T(8,128)(2,1)} %broadcast_in_dim.27), calls=%async_computation.1 | async-start | bytes 4194304 | tf_op jit(solution)/shard_map/all_to_all | solution.py:51
  39.8 2.7 %collective-permute-start.14 = (bf16[128,2048]{1,0:T(8,128)(2,1)S(1)}, bf16[128,2048]{1,0:T(8,128)(2,1)}, u32[]{:S(2)}, u32[]{:S(2)}) collective-permute-start(bf16[128,2048]{1,0:T(8,128)(2,1)S(1)} %collective-permute-done.3.refs_2_), channel_id=1, source_target_pairs={{0,224},{32,0},{64,32},{96,64},{128,96},{160,128},{192,160},{224,1... | collective-permute-start | bytes 1572872 | tf_op jit(solution)/shard_map/ppermute | solution.py:29
  42.5 1.4 collective-permute-start.5
  43.9 6.4 %collective-permute-done.4.refs_3_ = bf16[128,1280]{1,0:T(8,128)(2,1)} collective-permute-done((bf16[128,1280]{1,0:T(8,128)(2,1)S(1)}, bf16[128,1280]{1,0:T(8,128)(2,1)}, u32[]{:S(2)}, u32[]{:S(2)}) %collective-permute-start.4) | collective-permute-done | bytes 327712 | tf_op jit(solution)/shard_map/ppermute | solution.py:29
  50.3 1.2 collective-permute-start.13
  51.6 9.4 %collective-permute-done.5.refs_4_ = bf16[128,1280]{1,0:T(8,128)(2,1)} collective-permute-done((bf16[128,1280]{1,0:T(8,128)(2,1)S(1)}, bf16[128,1280]{1,0:T(8,128)(2,1)}, u32[]{:S(2)}, u32[]{:S(2)}) %collective-permute-start.5) | collective-permute-done | bytes 327712 | tf_op jit(solution)/shard_map/ppermute | solution.py:29
  61.0 3.1 %collective-permute-start.7 = (bf16[128,1280]{1,0:T(8,128)(2,1)}, bf16[128,1280]{1,0:T(8,128)(2,1)}, u32[]{:S(2)}, u32[]{:S(2)}) collective-permute-start(bf16[128,1280]{1,0:T(8,128)(2,1)} %collective-permute-done.5.refs_4_), channel_id=1, source_target_pairs={{0,224},{32,0},{64,32},{96,64},{128,96},{160,128},{192,160},{224,1... | collective-permute-start | bytes 983048 | tf_op jit(solution)/shard_map/ppermute | solution.py:29
  64.1 2.7 %collective-permute-start.16 = (bf16[128,2048]{1,0:T(8,128)(2,1)}, bf16[128,2048]{1,0:T(8,128)(2,1)}, u32[]{:S(2)}, u32[]{:S(2)}) collective-permute-start(bf16[128,2048]{1,0:T(8,128)(2,1)} %collective-permute-done.14.refs_4_), channel_id=1, source_target_pairs={{0,224},{32,0},{64,32},{96,64},{128,96},{160,128},{192,160},{224,1... | collective-permute-start | bytes 1572872 | tf_op jit(solution)/shard_map/ppermute | solution.py:29
  68.0 3.2 %collective-permute-done.7.refs_6_ = bf16[128,1280]{1,0:T(8,128)(2,1)} collective-permute-done((bf16[128,1280]{1,0:T(8,128)(2,1)}, bf16[128,1280]{1,0:T(8,128)(2,1)}, u32[]{:S(2)}, u32[]{:S(2)}) %collective-permute-start.7) | collective-permute-done | bytes 327712 | tf_op jit(solution)/shard_map/ppermute | solution.py:29
  71.2 7.3 %collective-permute-done.8.refs_7_ = bf16[128,1280]{1,0:T(8,128)(2,1)} collective-permute-done((bf16[128,1280]{1,0:T(8,128)(2,1)}, bf16[128,1280]{1,0:T(8,128)(2,1)}, u32[]{:S(2)}, u32[]{:S(2)}) %collective-permute-start.8) | collective-permute-done | bytes 327712 | tf_op jit(solution)/shard_map/ppermute | solution.py:29
  78.5 5.4 %partials.3 = (bf16[256,1280]{1,0:T(8,128)(2,1)}, bf16[256,1280]{1,0:T(8,128)(2,1)}, bf16[256,1280]{1,0:T(8,128)(2,1)S(1)}, f32[256,1280]{1,0:T(8,128)S(1)}) custom-call(s32[1]{0:T(128)} %bitcast.z_ref, bf16[1024,1024]{1,0:T(8,128)(2,1)S(1)} %dynamic-slice_dynamic-update-slice_fusion.cot_ref, bf16[128,1280]{1,0:T(8,128)(2,1)} %copy-done.7, ...), custom_call_target="tpu_custom_call" | custom-call | tf_op jit(solution)/shard_map/partials/pallas_call | solution.py:94
  83.9 0.8 copy-done
  84.8 1.3 collective-permute-start.10
  86.1 1.4 collective-permute-start.9
  87.5 2.7 %collective-permute-start.17 = (bf16[128,2048]{1,0:T(8,128)(2,1)}, bf16[128,2048]{1,0:T(8,128)(2,1)}, u32[]{:S(2)}, u32[]{:S(2)}) collective-permute-start(bf16[128,2048]{1,0:T(8,128)(2,1)} %collective-permute-done.16.refs_6_), channel_id=1, source_target_pairs={{0,224},{32,0},{64,32},{96,64},{128,96},{160,128},{192,160},{224,1... | collective-permute-start | bytes 1572872 | tf_op jit(solution)/shard_map/ppermute | solution.py:29
  91.0 0.7 fusion.26
  92.4 7.8 %collective-permute-done.15.refs_5_ = bf16[128,2048]{1,0:T(8,128)(2,1)} collective-permute-done((bf16[128,2048]{1,0:T(8,128)(2,1)}, bf16[128,2048]{1,0:T(8,128)(2,1)}, u32[]{:S(2)}, u32[]{:S(2)}) %collective-permute-start.15) | collective-permute-done | bytes 524320 | tf_op jit(solution)/shard_map/ppermute | solution.py:29
  100.2 4.2 %partials.5 = (bf16[256,1024]{1,0:T(8,128)(2,1)S(1)}, bf16[256,1024]{1,0:T(8,128)(2,1)S(1)}, bf16[256,1024]{1,0:T(8,128)(2,1)S(1)}, f32[256,1024]{1,0:T(8,128)S(1)}) custom-call(s32[1]{0:T(128)} %bitcast.z_ref, bf16[1024,1024]{1,0:T(8,128)(2,1)S(1)} %dynamic-slice_dynamic-update-slice_fusion.cot_ref, bf16[128,2048]{1,0:T(8,128)(2,1)} %copy-done.2, ...), custom_call_target="tpu_custom_call" | custom-call | tf_op jit(solution)/shard_map/partials/pallas_call | solution.py:94
  104.4 1.5 collective-permute-start.22
  106.0 1.2 add_convert_fusion.1
  107.3 2.7 %collective-permute-start.12 = (bf16[128,1280]{1,0:T(8,128)(2,1)S(1)}, bf16[128,1280]{1,0:T(8,128)(2,1)S(1)}, u32[]{:S(2)}, u32[]{:S(2)}) collective-permute-start(bf16[128,1280]{1,0:T(8,128)(2,1)S(1)} %get-tuple-element.42), channel_id=1, source_target_pairs={{0,24},{8,0},{16,8},{24,16},{1,25},{9,1},{17,9},{25,17},{2,26},{10... | collective-permute-start | bytes 983048 | tf_op jit(solution)/shard_map/ppermute | solution.py:29
  110.0 0.7 iota_compare_fusion
  110.7 4.2 %partials.4 = (bf16[256,1024]{1,0:T(8,128)(2,1)S(1)}, bf16[256,1024]{1,0:T(8,128)(2,1)S(1)}, bf16[256,1024]{1,0:T(8,128)(2,1)S(1)}, f32[256,1024]{1,0:T(8,128)S(1)}) custom-call(s32[1]{0:T(128)} %bitcast.z_ref, bf16[1024,1024]{1,0:T(8,128)(2,1)S(1)} %dynamic-slice_dynamic-update-slice_fusion.cot_ref, bf16[128,2048]{1,0:T(8,128)(2,1)} %copy-done.2, ...), custom_call_target="tpu_custom_call" | custom-call | tf_op jit(solution)/shard_map/partials/pallas_call | solution.py:94
  114.9 1.7 %collective-permute-start.18 = (bf16[256,1024]{1,0:T(8,128)(2,1)S(1)}, bf16[256,1024]{1,0:T(8,128)(2,1)S(1)}, u32[]{:S(2)}, u32[]{:S(2)}) collective-permute-start(bf16[256,1024]{1,0:T(8,128)(2,1)S(1)} %get-tuple-element.21), channel_id=1, source_target_pairs={{0,24},{8,0},{16,8},{24,16},{1,25},{9,1},{17,9},{25,17},{2,26},{10... | collective-permute-start | bytes 1572872 | tf_op jit(solution)/shard_map/ppermute | solution.py:29
  116.7 0.3 collective-permute-done.23
  117.3 1.3 slice.148
  118.7 1.0 slice.149
  119.7 4.4 %collective-permute-done.11 = bf16[128,1280]{1,0:T(8,128)(2,1)S(1)} collective-permute-done((bf16[128,1280]{1,0:T(8,128)(2,1)S(1)}, bf16[128,1280]{1,0:T(8,128)(2,1)S(1)}, u32[]{:S(2)}, u32[]{:S(2)}) %collective-permute-start.11) | collective-permute-done | bytes 327712 | tf_op jit(solution)/shard_map/ppermute | solution.py:29
  124.3 0.6 subtract_convert_fusion.3
  124.9 11.0 %collective-permute-start.26 = (bf16[256,256]{1,0:T(8,128)(2,1)S(1)}, bf16[256,256]{1,0:T(8,128)(2,1)S(1)}, u32[]{:S(2)}, u32[]{:S(2)}) collective-permute-start(bf16[256,256]{1,0:T(8,128)(2,1)S(1)} %slice.162), channel_id=1, source_target_pairs={{0,1},{1,2},{2,3},{3,4},{4,5},{5,6},{6,7},{8,9},{9,10},{10,11},{11... | collective-permute-start | bytes 393224 | tf_op jit(solution)/shard_map/ppermute | solution.py:184
  136.1 1.8 %collective-permute-start.20 = (bf16[128,1024]{1,0:T(8,128)(2,1)S(1)}, bf16[128,1024]{1,0:T(8,128)(2,1)S(1)}, u32[]{:S(2)}, u32[]{:S(2)}) collective-permute-start(bf16[128,1024]{1,0:T(8,128)(2,1)S(1)} %get-tuple-element.45), channel_id=1, source_target_pairs={{0,8},{8,16},{16,24},{24,0},{1,9},{9,17},{17,25},{25,1},{2,10},{10... | collective-permute-start | bytes 786440 | tf_op jit(solution)/shard_map/ppermute | solution.py:29
  137.9 0.9 collective-permute-start.21
  138.9 0.6 constant_dynamic-update-slice_fusion.2
  139.5 10.4 %collective-permute-start.27 = (bf16[256,256]{1,0:T(8,128)(2,1)S(1)}, bf16[256,256]{1,0:T(8,128)(2,1)S(1)}, u32[]{:S(2)}, u32[]{:S(2)}) collective-permute-start(bf16[256,256]{1,0:T(8,128)(2,1)S(1)} %slice.163), channel_id=1, source_target_pairs={{1,0},{2,1},{3,2},{4,3},{5,4},{6,5},{7,6},{9,8},{10,9},{11,10},{12... | collective-permute-start | bytes 393224 | tf_op jit(solution)/shard_map/ppermute | solution.py:185
  149.9 1.0 fusion.24
  151.0 1.0 fusion.25
  152.0 2.0 %pad_maximum_fusion = f32[256,3328]{1,0:T(8,128)} fusion(f32[256,640]{1,0:T(8,128)S(1)} %get-tuple-element.38, f32[256,1024]{1,0:T(8,128)S(1)} %get-tuple-element.31, f32[256,1024]{1,0:T(8,128)S(1)} %get-tuple-element.33, f32[256,640]{1,0:T(8,128)S(1)} %get-tuple-element.36), kind=kLoop, calls=%fused_computation | loop fusion | flops 2555904 | bytes 6815744 | tf_op jit(solution)/shard_map/concatenate | solution.py:191
  154.1 2.4 %dynamic-slice_select_fusion = bf16[256,3840]{1,0:T(8,128)(2,1)} fusion(bf16[256,4352]{1,0:T(8,128)(2,1)S(1)} %broadcast_dynamic-update-slice_fusion, s32[]{:T(128)S(6)} %select_n.79, pred[3840]{0:T(1024)(128)(4,1)S(1)} %iota_compare_fusion), kind=kLoop, calls=%fused_computation.1 | loop fusion | flops 983040 | bytes 3936004 | tf_op jit(solution)/shard_map/jit(_where)/select_n | solution.py:200
  (81 shorter events, 2.4 us)
Async XLA Ops:
  1.7 32.5 %copy-start.2 = (bf16[128,2048]{1,0:T(8,128)(2,1)}, bf16[128,2048]{1,0:T(8,128)(2,1)S(1)}, u32[]{:S(2)}) copy-start(bf16[128,2048]{1,0:T(8,128)(2,1)S(1)} %slice.114.refs_0_) | copy-start | bytes 1572868
  1.7 30.8 %collective-permute-start.2 = (bf16[128,2048]{1,0:T(8,128)(2,1)S(1)}, bf16[128,2048]{1,0:T(8,128)(2,1)}, u32[]{:S(2)}, u32[]{:S(2)}) collective-permute-start(bf16[128,2048]{1,0:T(8,128)(2,1)S(1)} %slice.114.refs_0_), channel_id=1, source_target_pairs={{0,32},{32,64},{64,96},{96,128},{128,160},{160,192},{192,224},{224... | collective-permute-start | bytes 1572872 | tf_op jit(solution)/shard_map/ppermute | solution.py:29
  4.3 28.3 %collective-permute-start.3 = (bf16[128,2048]{1,0:T(8,128)(2,1)S(1)}, bf16[128,2048]{1,0:T(8,128)(2,1)S(1)}, u32[]{:S(2)}, u32[]{:S(2)}) collective-permute-start(bf16[128,2048]{1,0:T(8,128)(2,1)S(1)} %slice.114.refs_0_), channel_id=1, source_target_pairs={{0,224},{32,0},{64,32},{96,64},{128,96},{160,128},{192,160},{224,1... | collective-permute-start | bytes 1572872 | tf_op jit(solution)/shard_map/ppermute | solution.py:29
  10.0 22.5 %all-to-all-start = ((bf16[16,8,1024]{2,0,1:T(8,128)(2,1)}), bf16[16,8,1024]{2,0,1:T(8,128)(2,1)S(1)}, u32[]{:S(2)}, u32[]{:S(2)}) async-start(bf16[16,8,1024]{2,0,1:T(8,128)(2,1)} %bitcast.13), calls=%async_computation | async-start | bytes 524288 | tf_op jit(solution)/shard_map/all_to_all | solution.py:147
  16.2 18.0 %copy-start.7 = (bf16[128,1280]{1,0:T(8,128)(2,1)}, bf16[128,1280]{1,0:T(8,128)(2,1)S(1)}, u32[]{:S(2)}) copy-start(bf16[128,1280]{1,0:T(8,128)(2,1)S(1)} %pad_maximum_fusion.1.refs_0_) | copy-start | bytes 983044
  16.2 16.3 %collective-permute-start = (bf16[128,1280]{1,0:T(8,128)(2,1)S(1)}, bf16[128,1280]{1,0:T(8,128)(2,1)S(1)}, u32[]{:S(2)}, u32[]{:S(2)}) collective-permute-start(bf16[128,1280]{1,0:T(8,128)(2,1)S(1)} %pad_maximum_fusion.1.refs_0_), channel_id=1, source_target_pairs={{0,32},{32,64},{64,96},{96,128},{128,160},{160,192},{192,224},{224... | collective-permute-start | bytes 983048 | tf_op jit(solution)/shard_map/ppermute | solution.py:29
  17.8 14.7 %collective-permute-start.1 = (bf16[128,1280]{1,0:T(8,128)(2,1)S(1)}, bf16[128,1280]{1,0:T(8,128)(2,1)S(1)}, u32[]{:S(2)}, u32[]{:S(2)}) collective-permute-start(bf16[128,1280]{1,0:T(8,128)(2,1)S(1)} %pad_maximum_fusion.1.refs_0_), channel_id=1, source_target_pairs={{0,224},{32,0},{64,32},{96,64},{128,96},{160,128},{192,160},{224,1... | collective-permute-start | bytes 983048 | tf_op jit(solution)/shard_map/ppermute | solution.py:29
  32.5 7.2 %copy-start.10 = (bf16[128,1280]{1,0:T(8,128)(2,1)}, bf16[128,1280]{1,0:T(8,128)(2,1)S(1)}, u32[]{:S(2)}) copy-start(bf16[128,1280]{1,0:T(8,128)(2,1)S(1)} %collective-permute-done.refs_1_) | copy-start | bytes 983044
  32.5 10.0 %copy-start.11 = (bf16[128,1280]{1,0:T(8,128)(2,1)}, bf16[128,1280]{1,0:T(8,128)(2,1)S(1)}, u32[]{:S(2)}) copy-start(bf16[128,1280]{1,0:T(8,128)(2,1)S(1)} %collective-permute-done.1.refs_2_) | copy-start | bytes 983044
  32.5 7.2 %copy-start.4 = (bf16[128,2048]{1,0:T(8,128)(2,1)}, bf16[128,2048]{1,0:T(8,128)(2,1)S(1)}, u32[]{:S(2)}) copy-start(bf16[128,2048]{1,0:T(8,128)(2,1)S(1)} %collective-permute-done.3.refs_2_) | copy-start | bytes 1572868
  34.2 32.6 %all-to-all-start.1 = ((bf16[8,128,1024]{2,1,0:T(8,128)(2,1)}), bf16[8,128,1024]{2,1,0:T(8,128)(2,1)S(1)}, u32[]{:S(2)}, u32[]{:S(2)}) async-start(bf16[8,128,1024]{2,1,0:T(8,128)(2,1)} %broadcast_in_dim.27), calls=%async_computation.1 | async-start | bytes 4194304 | tf_op jit(solution)/shard_map/all_to_all | solution.py:51
  39.7 10.6 %collective-permute-start.4 = (bf16[128,1280]{1,0:T(8,128)(2,1)S(1)}, bf16[128,1280]{1,0:T(8,128)(2,1)}, u32[]{:S(2)}, u32[]{:S(2)}) collective-permute-start(bf16[128,1280]{1,0:T(8,128)(2,1)S(1)} %collective-permute-done.refs_1_), channel_id=1, source_target_pairs={{0,32},{32,64},{64,96},{96,128},{128,160},{160,192},{192,224},{224... | collective-permute-start | bytes 983048 | tf_op jit(solution)/shard_map/ppermute | solution.py:29
  39.8 24.3 %collective-permute-start.14 = (bf16[128,2048]{1,0:T(8,128)(2,1)S(1)}, bf16[128,2048]{1,0:T(8,128)(2,1)}, u32[]{:S(2)}, u32[]{:S(2)}) collective-permute-start(bf16[128,2048]{1,0:T(8,128)(2,1)S(1)} %collective-permute-done.3.refs_2_), channel_id=1, source_target_pairs={{0,224},{32,0},{64,32},{96,64},{128,96},{160,128},{192,160},{224,1... | collective-permute-start | bytes 1572872 | tf_op jit(solution)/shard_map/ppermute | solution.py:29
  42.5 18.5 %collective-permute-start.5 = (bf16[128,1280]{1,0:T(8,128)(2,1)S(1)}, bf16[128,1280]{1,0:T(8,128)(2,1)}, u32[]{:S(2)}, u32[]{:S(2)}) collective-permute-start(bf16[128,1280]{1,0:T(8,128)(2,1)S(1)} %collective-permute-done.1.refs_2_), channel_id=1, source_target_pairs={{0,224},{32,0},{64,32},{96,64},{128,96},{160,128},{192,160},{224,1... | collective-permute-start | bytes 983048 | tf_op jit(solution)/shard_map/ppermute | solution.py:29
  50.3 13.7 %collective-permute-start.6 = (bf16[128,1280]{1,0:T(8,128)(2,1)}, bf16[128,1280]{1,0:T(8,128)(2,1)}, u32[]{:S(2)}, u32[]{:S(2)}) collective-permute-start(bf16[128,1280]{1,0:T(8,128)(2,1)} %collective-permute-done.4.refs_3_), channel_id=1, source_target_pairs={{0,32},{32,64},{64,96},{96,128},{128,160},{160,192},{192,224},{224... | collective-permute-start | bytes 983048 | tf_op jit(solution)/shard_map/ppermute | solution.py:29
  50.3 37.2 %collective-permute-start.13 = (bf16[128,2048]{1,0:T(8,128)(2,1)}, bf16[128,2048]{1,0:T(8,128)(2,1)}, u32[]{:S(2)}, u32[]{:S(2)}) collective-permute-start(bf16[128,2048]{1,0:T(8,128)(2,1)} %collective-permute-done.2.refs_1_), channel_id=1, source_target_pairs={{0,32},{32,64},{64,96},{96,128},{128,160},{160,192},{192,224},{224... | collective-permute-start | bytes 1572872 | tf_op jit(solution)/shard_map/ppermute | solution.py:29
  61.0 10.2 %collective-permute-start.7 = (bf16[128,1280]{1,0:T(8,128)(2,1)}, bf16[128,1280]{1,0:T(8,128)(2,1)}, u32[]{:S(2)}, u32[]{:S(2)}) collective-permute-start(bf16[128,1280]{1,0:T(8,128)(2,1)} %collective-permute-done.5.refs_4_), channel_id=1, source_target_pairs={{0,224},{32,0},{64,32},{96,64},{128,96},{160,128},{192,160},{224,1... | collective-permute-start | bytes 983048 | tf_op jit(solution)/shard_map/ppermute | solution.py:29
  64.1 14.4 %collective-permute-start.8 = (bf16[128,1280]{1,0:T(8,128)(2,1)}, bf16[128,1280]{1,0:T(8,128)(2,1)}, u32[]{:S(2)}, u32[]{:S(2)}) collective-permute-start(bf16[128,1280]{1,0:T(8,128)(2,1)} %collective-permute-done.6.refs_5_), channel_id=1, source_target_pairs={{0,32},{32,64},{64,96},{96,128},{128,160},{160,192},{192,224},{224... | collective-permute-start | bytes 983048 | tf_op jit(solution)/shard_map/ppermute | solution.py:29
  64.1 23.4 %collective-permute-start.16 = (bf16[128,2048]{1,0:T(8,128)(2,1)}, bf16[128,2048]{1,0:T(8,128)(2,1)}, u32[]{:S(2)}, u32[]{:S(2)}) collective-permute-start(bf16[128,2048]{1,0:T(8,128)(2,1)} %collective-permute-done.14.refs_4_), channel_id=1, source_target_pairs={{0,224},{32,0},{64,32},{96,64},{128,96},{160,128},{192,160},{224,1... | collective-permute-start | bytes 1572872 | tf_op jit(solution)/shard_map/ppermute | solution.py:29
  78.5 12.5 %copy-start.12 = (s32[8]{0:T(128)S(1)}, s32[8]{0:T(128)}, u32[]{:S(2)}) copy-start(s32[8]{0:T(128)} %param.12) | copy-start | bytes 100
  83.9 0.8 copy-start
  84.8 21.2 %collective-permute-start.10 = (bf16[256,1280]{1,0:T(8,128)(2,1)}, bf16[256,1280]{1,0:T(8,128)(2,1)}, u32[]{:S(2)}, u32[]{:S(2)}) collective-permute-start(bf16[256,1280]{1,0:T(8,128)(2,1)} %get-tuple-element.18), channel_id=1, source_target_pairs={{0,8},{8,16},{16,24},{24,0},{1,9},{9,17},{17,25},{25,1},{2,10},{10... | collective-permute-start | bytes 1966088 | tf_op jit(solution)/shard_map/ppermute | solution.py:29
  86.1 19.9 %collective-permute-start.9 = (bf16[256,1280]{1,0:T(8,128)(2,1)}, bf16[256,1280]{1,0:T(8,128)(2,1)}, u32[]{:S(2)}, u32[]{:S(2)}) collective-permute-start(bf16[256,1280]{1,0:T(8,128)(2,1)} %get-tuple-element.17), channel_id=1, source_target_pairs={{0,24},{8,0},{16,8},{24,16},{1,25},{9,1},{17,9},{25,17},{2,26},{10... | collective-permute-start | bytes 1966088 | tf_op jit(solution)/shard_map/ppermute | solution.py:29
  87.5 12.7 %collective-permute-start.15 = (bf16[128,2048]{1,0:T(8,128)(2,1)}, bf16[128,2048]{1,0:T(8,128)(2,1)}, u32[]{:S(2)}, u32[]{:S(2)}) collective-permute-start(bf16[128,2048]{1,0:T(8,128)(2,1)} %collective-permute-done.13.refs_3_), channel_id=1, source_target_pairs={{0,32},{32,64},{64,96},{96,128},{128,160},{160,192},{192,224},{224... | collective-permute-start | bytes 1572872 | tf_op jit(solution)/shard_map/ppermute | solution.py:29
  87.5 12.7 %collective-permute-start.17 = (bf16[128,2048]{1,0:T(8,128)(2,1)}, bf16[128,2048]{1,0:T(8,128)(2,1)}, u32[]{:S(2)}, u32[]{:S(2)}) collective-permute-start(bf16[128,2048]{1,0:T(8,128)(2,1)} %collective-permute-done.16.refs_6_), channel_id=1, source_target_pairs={{0,224},{32,0},{64,32},{96,64},{128,96},{160,128},{192,160},{224,1... | collective-permute-start | bytes 1572872 | tf_op jit(solution)/shard_map/ppermute | solution.py:29
  92.4 13.6 %copy-start.1 = (bf16[256,1280]{1,0:T(8,128)(2,1)S(1)}, bf16[256,1280]{1,0:T(8,128)(2,1)}, u32[]{:S(2)}) copy-start(bf16[256,1280]{1,0:T(8,128)(2,1)} %copy-done) | copy-start | bytes 1966084
  104.4 12.2 %collective-permute-start.22 = (bf16[256,1024]{1,0:T(8,128)(2,1)S(1)}, bf16[256,1024]{1,0:T(8,128)(2,1)S(1)}, u32[]{:S(2)}, u32[]{:S(2)}) collective-permute-start(bf16[256,1024]{1,0:T(8,128)(2,1)S(1)} %get-tuple-element.25), channel_id=1, source_target_pairs={{0,24},{8,0},{16,8},{24,16},{1,25},{9,1},{17,9},{25,17},{2,26},{10... | collective-permute-start | bytes 1572872 | tf_op jit(solution)/shard_map/ppermute | solution.py:29
  105.9 11.1 %collective-permute-start.23 = (bf16[256,1024]{1,0:T(8,128)(2,1)S(1)}, bf16[256,1024]{1,0:T(8,128)(2,1)S(1)}, u32[]{:S(2)}, u32[]{:S(2)}) collective-permute-start(bf16[256,1024]{1,0:T(8,128)(2,1)S(1)} %get-tuple-element.26), channel_id=1, source_target_pairs={{0,8},{8,16},{16,24},{24,0},{1,9},{9,17},{17,25},{25,1},{2,10},{10... | collective-permute-start | bytes 1572872 | tf_op jit(solution)/shard_map/ppermute | solution.py:29
  107.2 16.8 %collective-permute-start.11 = (bf16[128,1280]{1,0:T(8,128)(2,1)S(1)}, bf16[128,1280]{1,0:T(8,128)(2,1)S(1)}, u32[]{:S(2)}, u32[]{:S(2)}) collective-permute-start(bf16[128,1280]{1,0:T(8,128)(2,1)S(1)} %get-tuple-element.41), channel_id=1, source_target_pairs={{0,8},{8,16},{16,24},{24,0},{1,9},{9,17},{17,25},{25,1},{2,10},{10... | collective-permute-start | bytes 983048 | tf_op jit(solution)/shard_map/ppermute | solution.py:29
  107.3 16.7 %collective-permute-start.12 = (bf16[128,1280]{1,0:T(8,128)(2,1)S(1)}, bf16[128,1280]{1,0:T(8,128)(2,1)S(1)}, u32[]{:S(2)}, u32[]{:S(2)}) collective-permute-start(bf16[128,1280]{1,0:T(8,128)(2,1)S(1)} %get-tuple-element.42), channel_id=1, source_target_pairs={{0,24},{8,0},{16,8},{24,16},{1,25},{9,1},{17,9},{25,17},{2,26},{10... | collective-permute-start | bytes 983048 | tf_op jit(solution)/shard_map/ppermute | solution.py:29
  114.9 20.9 %collective-permute-start.18 = (bf16[256,1024]{1,0:T(8,128)(2,1)S(1)}, bf16[256,1024]{1,0:T(8,128)(2,1)S(1)}, u32[]{:S(2)}, u32[]{:S(2)}) collective-permute-start(bf16[256,1024]{1,0:T(8,128)(2,1)S(1)} %get-tuple-element.21), channel_id=1, source_target_pairs={{0,24},{8,0},{16,8},{24,16},{1,25},{9,1},{17,9},{25,17},{2,26},{10... | collective-permute-start | bytes 1572872 | tf_op jit(solution)/shard_map/ppermute | solution.py:29
  116.6 22.3 %copy-start.8 = (bf16[256,1024]{1,0:T(8,128)(2,1)}, bf16[256,1024]{1,0:T(8,128)(2,1)S(1)}, u32[]{:S(2)}) copy-start(bf16[256,1024]{1,0:T(8,128)(2,1)S(1)} %collective-permute-done.22) | copy-start | bytes 1572868
  116.6 19.2 %collective-permute-start.19 = (bf16[256,1024]{1,0:T(8,128)(2,1)S(1)}, bf16[256,1024]{1,0:T(8,128)(2,1)S(1)}, u32[]{:S(2)}, u32[]{:S(2)}) collective-permute-start(bf16[256,1024]{1,0:T(8,128)(2,1)S(1)} %get-tuple-element.22), channel_id=1, source_target_pairs={{0,8},{8,16},{16,24},{24,0},{1,9},{9,17},{17,25},{25,1},{2,10},{10... | collective-permute-start | bytes 1572872 | tf_op jit(solution)/shard_map/ppermute | solution.py:29
  117.0 21.9 %copy-start.9 = (bf16[256,1024]{1,0:T(8,128)(2,1)}, bf16[256,1024]{1,0:T(8,128)(2,1)S(1)}, u32[]{:S(2)}) copy-start(bf16[256,1024]{1,0:T(8,128)(2,1)S(1)} %collective-permute-done.23) | copy-start | bytes 1572868
  117.0 7.2 %copy-start.6 = (bf16[256,3328]{1,0:T(8,128)(2,1)S(1)}, bf16[256,3328]{1,0:T(8,128)(2,1)}, u32[]{:S(2)}) copy-start(bf16[256,3328]{1,0:T(8,128)(2,1)} %param.10) | copy-start | bytes 5111812
  117.2 33.7 %collective-permute-start.24 = (bf16[128,1024]{1,0:T(8,128)(2,1)S(1)}, bf16[128,1024]{1,0:T(8,128)(2,1)S(1)}, u32[]{:S(2)}, u32[]{:S(2)}) collective-permute-start(bf16[128,1024]{1,0:T(8,128)(2,1)S(1)} %get-tuple-element.43), channel_id=1, source_target_pairs={{0,8},{8,16},{16,24},{24,0},{1,9},{9,17},{17,25},{25,1},{2,10},{10... | collective-permute-start | bytes 786440 | tf_op jit(solution)/shard_map/ppermute | solution.py:29
  117.3 7.0 %copy-start.5 = (bf16[256,3328]{1,0:T(8,128)(2,1)S(1)}, bf16[256,3328]{1,0:T(8,128)(2,1)}, u32[]{:S(2)}) copy-start(bf16[256,3328]{1,0:T(8,128)(2,1)} %param.11) | copy-start | bytes 5111812
  119.7 4.6 %copy-start.3 = (f32[256,3328]{1,0:T(8,128)S(1)}, f32[256,3328]{1,0:T(8,128)}, u32[]{:S(2)}) copy-start(f32[256,3328]{1,0:T(8,128)} %param.9) | copy-start | bytes 10223620
  124.1 26.9 %collective-permute-start.25 = (bf16[128,1024]{1,0:T(8,128)(2,1)S(1)}, bf16[128,1024]{1,0:T(8,128)(2,1)S(1)}, u32[]{:S(2)}, u32[]{:S(2)}) collective-permute-start(bf16[128,1024]{1,0:T(8,128)(2,1)S(1)} %get-tuple-element.44), channel_id=1, source_target_pairs={{0,24},{8,0},{16,8},{24,16},{1,25},{9,1},{17,9},{25,17},{2,26},{10... | collective-permute-start | bytes 786440 | tf_op jit(solution)/shard_map/ppermute | solution.py:29
  124.9 14.0 %collective-permute-start.26 = (bf16[256,256]{1,0:T(8,128)(2,1)S(1)}, bf16[256,256]{1,0:T(8,128)(2,1)S(1)}, u32[]{:S(2)}, u32[]{:S(2)}) collective-permute-start(bf16[256,256]{1,0:T(8,128)(2,1)S(1)} %slice.162), channel_id=1, source_target_pairs={{0,1},{1,2},{2,3},{3,4},{4,5},{5,6},{6,7},{8,9},{9,10},{10,11},{11... | collective-permute-start | bytes 393224 | tf_op jit(solution)/shard_map/ppermute | solution.py:184
  136.1 13.8 %collective-permute-start.20 = (bf16[128,1024]{1,0:T(8,128)(2,1)S(1)}, bf16[128,1024]{1,0:T(8,128)(2,1)S(1)}, u32[]{:S(2)}, u32[]{:S(2)}) collective-permute-start(bf16[128,1024]{1,0:T(8,128)(2,1)S(1)} %get-tuple-element.45), channel_id=1, source_target_pairs={{0,8},{8,16},{16,24},{24,0},{1,9},{9,17},{17,25},{25,1},{2,10},{10... | collective-permute-start | bytes 786440 | tf_op jit(solution)/shard_map/ppermute | solution.py:29
  137.9 12.0 %collective-permute-start.21 = (bf16[128,1024]{1,0:T(8,128)(2,1)S(1)}, bf16[128,1024]{1,0:T(8,128)(2,1)S(1)}, u32[]{:S(2)}, u32[]{:S(2)}) collective-permute-start(bf16[128,1024]{1,0:T(8,128)(2,1)S(1)} %get-tuple-element.46), channel_id=1, source_target_pairs={{0,24},{8,0},{16,8},{24,16},{1,25},{9,1},{17,9},{25,17},{2,26},{10... | collective-permute-start | bytes 786440 | tf_op jit(solution)/shard_map/ppermute | solution.py:29
  139.5 14.5 %collective-permute-start.27 = (bf16[256,256]{1,0:T(8,128)(2,1)S(1)}, bf16[256,256]{1,0:T(8,128)(2,1)S(1)}, u32[]{:S(2)}, u32[]{:S(2)}) collective-permute-start(bf16[256,256]{1,0:T(8,128)(2,1)S(1)} %slice.163), channel_id=1, source_target_pairs={{1,0},{2,1},{3,2},{4,3},{5,4},{6,5},{7,6},{9,8},{10,9},{11,10},{12... | collective-permute-start | bytes 393224 | tf_op jit(solution)/shard_map/ppermute | solution.py:185
  149.9 1.1 slice-start
  149.9 1.1 slice-start.1

commit v3 on v2

--- a/solution.py
+++ b/solution.py
@@ -14,7 +14,9 @@
 N_Y = 4
 N_X = 4
 LEFT = 640
+MIDDLE = 1664
 RIGHT = 2688
+SPAN = 512
 
 beta_first = 0.9
 beta_second = 0.95
@@ -82,31 +84,32 @@
         low += size
 
 
-def partials(z, cotangent, pieces, low, cols, tile):
+def half_partials(z, cotangent, pieces, low, cols, tile, which, kinds):
     tokens, features = cotangent.shape
     rows = features // N_Y
     first = low // tile
     along = lambda i: (0, i)
     shifted = lambda i: (0, i + first)
-    sizes = (rows, rows, rows, rows)
-    kinds = (jnp.bfloat16, jnp.bfloat16, jnp.bfloat16, jnp.float32)
     body = functools.partial(partials_body, tuple(p[1] for p in pieces))
     return pl.pallas_call(
         body,
         grid=(cols // tile,),
         in_specs=[
             pl.BlockSpec(memory_space=pltpu.SMEM),
-            pl.BlockSpec(cotangent.shape, lambda i: (0, 0)),
+            pl.BlockSpec((tokens, 2 * rows), lambda i: (0, which)),
         ]
         + [pl.BlockSpec((p[0].shape[0], tile), shifted) for p in pieces],
-        out_specs=[pl.BlockSpec((size, tile), along) for size in sizes],
-        out_shape=[
-            jax.ShapeDtypeStruct((size, cols), kind) for size, kind in zip(sizes, kinds)
-        ],
+        out_specs=[pl.BlockSpec((rows, tile), along) for _ in kinds],
+        out_shape=[jax.ShapeDtypeStruct((rows, cols), kind) for kind in kinds],
         scratch_shapes=[pltpu.VMEM((tokens, tile), jnp.bfloat16)],
-        compiler_params=pltpu.CompilerParams(vmem_limit_bytes=20 * 1024 * 1024),
+        compiler_params=pltpu.CompilerParams(vmem_limit_bytes=16 * 1024 * 1024),
         name="partials",
     )(z, cotangent, *[pltpu.with_memory_space_constraint(p[0], pltpu.HBM) for p in pieces])
+
+
+def partials(z, cotangent, pieces, low, cols, tile):
+    take = functools.partial(half_partials, z, cotangent, pieces, low, cols, tile)
+    return *take(0, (jnp.bfloat16, jnp.bfloat16)), *take(1, (jnp.bfloat16, jnp.float32))
 
 
 def ring_scatter(part):
@@ -157,9 +160,10 @@
     rim_gradient = ring_scatter(
         partials(z, cotangent, rim_pieces, 0, rim.shape[1], rim.shape[1] // 2)
     )
-    span = (RIGHT - LEFT) // 2
-    first_gradient = ring_scatter(partials(z, cotangent, inner_pieces, 0, span, span // 2))
-    second_gradient = ring_scatter(partials(z, cotangent, inner_pieces, span, span, span // 2))
+    span = MIDDLE - LEFT
+    rest = RIGHT - MIDDLE
+    first_gradient = ring_scatter(partials(z, cotangent, inner_pieces, 0, span, SPAN))
+    second_gradient = ring_scatter(partials(z, cotangent, inner_pieces, span, rest, SPAN))
 
     updates = {}
     weights = {}
@@ -183,12 +187,13 @@
     last = tensor_count - 1
     left = lax.ppermute(tail, TENSOR, [(i, i + 1) for i in range(last)])
     right = lax.ppermute(head, TENSOR, [(i + 1, i) for i in range(last)])
-    blank = jnp.zeros((rows, 2 * DRIFT), jnp.bfloat16)
-    order = sorted(weights)
-    widened = jnp.concatenate(
-        [left] + [weights[k] for k in order] + [right, blank], axis=1
-    )
-    update = jnp.concatenate([updates[k] for k in order], axis=1)
+    widened = jnp.zeros((rows, width + 4 * DRIFT), jnp.bfloat16)
+    widened = lax.dynamic_update_slice(widened, left, (0, 0))
+    widened = lax.dynamic_update_slice(widened, right, (0, width + DRIFT))
+    update = jnp.zeros((rows, width), jnp.float32)
+    for low in weights:
+        update = lax.dynamic_update_slice(update, updates[low], (0, low))
+        widened = lax.dynamic_update_slice(widened, weights[low], (0, low + DRIFT))
 
     position = lax.axis_index(TENSOR)
     places = jnp.arange(tensor_count, dtype=jnp.int32)

time: 157 us -> 154 us (0.981); the launches traced: 156 us -> 152 us
  starting transfers between devices: 66.9 us -> 58.6 us
  Pallas kernels: 13.9 us -> 19.7 us
  other arithmetic: 10.8 us -> 8.59 us
    ppermute x1, starting transfers between devices: 10.4 us -> 1.96 us  [per_device(): right = lax.ppermute(head, TENSOR, [(i + 1, i) for i in range(last)])]
    pallas_call x3 -> x6, Pallas kernels: 13.9 us -> 19.7 us  [half_partials(): pl.pallas_call(body, grid=(cols // tile,), in_specs=[pl.BlockSpec(memory_...]
    ppermute x26, starting transfers between devices: 34.9 us -> 38.1 us  [shift(): lax.ppermute(value, axis, [(i, (i + by) % count) for i in range(count)])]
    ppermute x1, starting transfers between devices: 11 us -> 7.76 us  [per_device(): left = lax.ppermute(tail, TENSOR, [(i, i + 1) for i in range(last)])]
    unnamed x3 -> x0, other arithmetic: 2.61 us -> none
    dynamic_update_slice x0 -> x2, other arithmetic: none -> 2.02 us  [per_device(): widened = lax.dynamic_update_slice(widened, weights[low], (0, low + DRIFT))]
    concatenate x1 -> x0, other arithmetic: 2 us -> none  [per_device(): update = jnp.concatenate([updates[k] for k in order], axis=1)]
    ppermute x26, waiting for transfers between devices: 52.3 us -> 50.6 us  [shift(): lax.ppermute(value, axis, [(i, (i + by) % count) for i in range(count)])]
  transfers between devices with their start and end apart: 30 -> 30, of which waited for: 8 -> 9; matrix products, arithmetic and copies ran while one was open for 9% -> 8% of each run, Pallas kernels for 9% -> 13%
where the time goes in v3:
time: 154 us; the launch traced here: 152 us
  starting transfers between devices  58.6 us (38%)
  waiting for transfers between devices  51.4 us (33%)
  Pallas kernels  19.7 us (13%)
  local copies, waits for them, and re-layouts  10.8 us (7%)
  other arithmetic  8.59 us (6%)
  between operations  2.57 us (2%)
    ppermute x26, waiting for transfers between devices, shift(): lax.ppermute(value, axis, [(i, (i + by) % count) for i in range(count)])  50.6 us
    ppermute x26, starting transfers between devices, shift(): lax.ppermute(value, axis, [(i, (i + by) % count) for i in range(count)])  38.1 us
    pallas_call x6, Pallas kernels, half_partials(): pl.pallas_call(body, grid=(cols // tile,), in_specs=[pl.BlockSpec(memory_...  19.7 us
    ppermute x1, starting transfers between devices, per_device(): left = lax.ppermute(tail, TENSOR, [(i, i + 1) for i in range(last)])  7.76 us
    all_to_all x1, starting transfers between devices, cotangent_of(): lax.all_to_all(copies, TENSOR, split_axis=0, concat_axis=0, tiled=True)  5.52 us
    all_to_all x1, starting transfers between devices, per_device(): lax.all_to_all(out_grad, 'z', split_axis=1, concat_axis=0, tiled=True)  5.2 us
    slice x10, local copies, waits for them, and re-layouts, ring_scatter(): direct = jnp.concatenate([above[half:], below[half:]], axis=0).astype(wide)  3.26 us
  transfers between devices with their start and end apart: 30, of which 9 were waited for; matrix products, arithmetic and copies ran while one was open for 8% of the time, Pallas kernels for 13%

profile of v3, /device:TPU:1, one launch (start us, length us, event | category | flops | bytes accessed | tf_op | source)
XLA Modules:
  0.0 151.6 jit_solution(5799657348661972499)
XLA Ops:
  0.6 1.1 slice.114.refs_0_
  1.7 2.5 %collective-permute-start.2 = (bf16[128,2048]{1,0:T(8,128)(2,1)S(1)}, bf16[128,2048]{1,0:T(8,128)(2,1)}, u32[]{:S(2)}, u32[]{:S(2)}) collective-permute-start(bf16[128,2048]{1,0:T(8,128)(2,1)S(1)} %slice.114.refs_0_), channel_id=1, source_target_pairs={{0,32},{32,64},{64,96},{96,128},{128,160},{160,192},{192,224},{224... | collective-permute-start | bytes 1572872 | tf_op jit(solution)/shard_map/ppermute | solution.py:31
  4.3 4.0 %collective-permute-start.3 = (bf16[128,2048]{1,0:T(8,128)(2,1)S(1)}, bf16[128,2048]{1,0:T(8,128)(2,1)S(1)}, u32[]{:S(2)}, u32[]{:S(2)}) collective-permute-start(bf16[128,2048]{1,0:T(8,128)(2,1)S(1)} %slice.114.refs_0_), channel_id=1, source_target_pairs={{0,224},{32,0},{64,32},{96,64},{128,96},{160,128},{192,160},{224,1... | collective-permute-start | bytes 1572872 | tf_op jit(solution)/shard_map/ppermute | solution.py:31
  8.3 1.7 %copy.16 = bf16[2,8,8,1024]{3,2,0,1:T(8,128)(2,1)} copy(bf16[2,8,8,1024]{3,2,1,0:T(8,128)(2,1)} %bitcast.24) | data formatting | bytes 524288 | tf_op jit(solution)/shard_map/all_to_all | solution.py:150
  10.0 5.2 %all-to-all-start = ((bf16[16,8,1024]{2,0,1:T(8,128)(2,1)}), bf16[16,8,1024]{2,0,1:T(8,128)(2,1)S(1)}, u32[]{:S(2)}, u32[]{:S(2)}) async-start(bf16[16,8,1024]{2,0,1:T(8,128)(2,1)} %bitcast.13), calls=%async_computation | async-start | bytes 524288 | tf_op jit(solution)/shard_map/all_to_all | solution.py:150
  15.2 1.0 fusion.28
  16.2 1.5 %collective-permute-start = (bf16[128,1280]{1,0:T(8,128)(2,1)S(1)}, bf16[128,1280]{1,0:T(8,128)(2,1)S(1)}, u32[]{:S(2)}, u32[]{:S(2)}) collective-permute-start(bf16[128,1280]{1,0:T(8,128)(2,1)S(1)} %pad_maximum_fusion.refs_0_), channel_id=1, source_target_pairs={{0,32},{32,64},{64,96},{96,128},{128,160},{160,192},{192,224},{224... | collective-permute-start | bytes 983048 | tf_op jit(solution)/shard_map/ppermute | solution.py:31
  17.8 1.8 %collective-permute-start.1 = (bf16[128,1280]{1,0:T(8,128)(2,1)S(1)}, bf16[128,1280]{1,0:T(8,128)(2,1)S(1)}, u32[]{:S(2)}, u32[]{:S(2)}) collective-permute-start(bf16[128,1280]{1,0:T(8,128)(2,1)S(1)} %pad_maximum_fusion.refs_0_), channel_id=1, source_target_pairs={{0,224},{32,0},{64,32},{96,64},{128,96},{160,128},{192,160},{224,1... | collective-permute-start | bytes 983048 | tf_op jit(solution)/shard_map/ppermute | solution.py:31
  19.6 12.9 %collective-permute-done.refs_1_ = bf16[128,1280]{1,0:T(8,128)(2,1)S(1)} collective-permute-done((bf16[128,1280]{1,0:T(8,128)(2,1)S(1)}, bf16[128,1280]{1,0:T(8,128)(2,1)S(1)}, u32[]{:S(2)}, u32[]{:S(2)}) %collective-permute-start) | collective-permute-done | bytes 327712 | tf_op jit(solution)/shard_map/ppermute | solution.py:31
  32.5 1.7 %broadcast_in_dim.26 = bf16[8,128,1024]{2,1,0:T(8,128)(2,1)} broadcast(bf16[128,1024]{1,0:T(8,128)(2,1)S(1)} %bitcast.23), dimensions={1,2} | broadcast | bytes 2359296 | tf_op jit(solution)/shard_map/broadcast_in_dim | solution.py:52
  34.2 5.5 %all-to-all-start.1 = ((bf16[8,128,1024]{2,1,0:T(8,128)(2,1)}), bf16[8,128,1024]{2,1,0:T(8,128)(2,1)S(1)}, u32[]{:S(2)}, u32[]{:S(2)}) async-start(bf16[8,128,1024]{2,1,0:T(8,128)(2,1)} %broadcast_in_dim.26), calls=%async_computation.1 | async-start | bytes 4194304 | tf_op jit(solution)/shard_map/all_to_all | solution.py:53
  39.8 2.7 %collective-permute-start.14 = (bf16[128,2048]{1,0:T(8,128)(2,1)S(1)}, bf16[128,2048]{1,0:T(8,128)(2,1)}, u32[]{:S(2)}, u32[]{:S(2)}) collective-permute-start(bf16[128,2048]{1,0:T(8,128)(2,1)S(1)} %collective-permute-done.3.refs_2_), channel_id=1, source_target_pairs={{0,224},{32,0},{64,32},{96,64},{128,96},{160,128},{192,160},{224,1... | collective-permute-start | bytes 1572872 | tf_op jit(solution)/shard_map/ppermute | solution.py:31
  42.5 1.4 collective-permute-start.5
  43.9 6.4 %collective-permute-done.4.refs_3_ = bf16[128,1280]{1,0:T(8,128)(2,1)} collective-permute-done((bf16[128,1280]{1,0:T(8,128)(2,1)S(1)}, bf16[128,1280]{1,0:T(8,128)(2,1)}, u32[]{:S(2)}, u32[]{:S(2)}) %collective-permute-start.4) | collective-permute-done | bytes 327712 | tf_op jit(solution)/shard_map/ppermute | solution.py:31
  50.3 1.2 collective-permute-start.13
  51.6 9.4 %collective-permute-done.5.refs_4_ = bf16[128,1280]{1,0:T(8,128)(2,1)} collective-permute-done((bf16[128,1280]{1,0:T(8,128)(2,1)S(1)}, bf16[128,1280]{1,0:T(8,128)(2,1)}, u32[]{:S(2)}, u32[]{:S(2)}) %collective-permute-start.5) | collective-permute-done | bytes 327712 | tf_op jit(solution)/shard_map/ppermute | solution.py:31
  61.0 3.1 %collective-permute-start.7 = (bf16[128,1280]{1,0:T(8,128)(2,1)}, bf16[128,1280]{1,0:T(8,128)(2,1)S(1)}, u32[]{:S(2)}, u32[]{:S(2)}) collective-permute-start(bf16[128,1280]{1,0:T(8,128)(2,1)} %collective-permute-done.5.refs_4_), channel_id=1, source_target_pairs={{0,224},{32,0},{64,32},{96,64},{128,96},{160,128},{192,160},{224,1... | collective-permute-start | bytes 983048 | tf_op jit(solution)/shard_map/ppermute | solution.py:31
  64.1 2.7 %collective-permute-start.16 = (bf16[128,2048]{1,0:T(8,128)(2,1)}, bf16[128,2048]{1,0:T(8,128)(2,1)}, u32[]{:S(2)}, u32[]{:S(2)}) collective-permute-start(bf16[128,2048]{1,0:T(8,128)(2,1)} %collective-permute-done.14.refs_4_), channel_id=1, source_target_pairs={{0,224},{32,0},{64,32},{96,64},{128,96},{160,128},{192,160},{224,1... | collective-permute-start | bytes 1572872 | tf_op jit(solution)/shard_map/ppermute | solution.py:31
  68.0 3.2 %collective-permute-done.7.refs_6_ = bf16[128,1280]{1,0:T(8,128)(2,1)S(1)} collective-permute-done((bf16[128,1280]{1,0:T(8,128)(2,1)}, bf16[128,1280]{1,0:T(8,128)(2,1)S(1)}, u32[]{:S(2)}, u32[]{:S(2)}) %collective-permute-start.7) | collective-permute-done | bytes 327712 | tf_op jit(solution)/shard_map/ppermute | solution.py:31
  71.2 7.3 %collective-permute-done.8.refs_7_ = bf16[128,1280]{1,0:T(8,128)(2,1)} collective-permute-done((bf16[128,1280]{1,0:T(8,128)(2,1)S(1)}, bf16[128,1280]{1,0:T(8,128)(2,1)}, u32[]{:S(2)}, u32[]{:S(2)}) %collective-permute-start.8) | collective-permute-done | bytes 327712 | tf_op jit(solution)/shard_map/ppermute | solution.py:31
  78.5 3.8 %partials.7 = (bf16[256,1280]{1,0:T(8,128)(2,1)S(1)}, bf16[256,1280]{1,0:T(8,128)(2,1)S(1)}) custom-call(s32[1]{0:T(128)} %bitcast.z_ref, bf16[1024,1024]{1,0:T(8,128)(2,1)S(1)} %dynamic-slice_dynamic-update-slice_fusion.cot_ref, bf16[128,1280]{1,0:T(8,128)(2,1)} %copy-done.4, bf16[128,1280]{1,0:T(8,128)(2,1)} %copy-done.7, bf16[128,1280]{1,0:T(8,128)(2,1)} %copy-done.8, ...), custom_call_target="tpu_custom_call" | custom-call | tf_op jit(solution)/shard_map/partials/pallas_call | solution.py:94
  82.3 1.4 collective-permute-start.10
  83.6 1.5 %collective-permute-start.9 = (bf16[256,1280]{1,0:T(8,128)(2,1)S(1)}, bf16[256,1280]{1,0:T(8,128)(2,1)}, u32[]{:S(2)}, u32[]{:S(2)}) collective-permute-start(bf16[256,1280]{1,0:T(8,128)(2,1)S(1)} %get-tuple-element.17), channel_id=1, source_target_pairs={{0,24},{8,0},{16,8},{24,16},{1,25},{9,1},{17,9},{25,17},{2,26},{10... | collective-permute-start | bytes 1966088 | tf_op jit(solution)/shard_map/ppermute | solution.py:31
  85.2 2.7 %collective-permute-start.17 = (bf16[128,2048]{1,0:T(8,128)(2,1)}, bf16[128,2048]{1,0:T(8,128)(2,1)}, u32[]{:S(2)}, u32[]{:S(2)}) collective-permute-start(bf16[128,2048]{1,0:T(8,128)(2,1)} %collective-permute-done.16.refs_6_), channel_id=1, source_target_pairs={{0,224},{32,0},{64,32},{96,64},{128,96},{160,128},{192,160},{224,1... | collective-permute-start | bytes 1572872 | tf_op jit(solution)/shard_map/ppermute | solution.py:31
  88.6 0.6 fusion.26
  89.9 8.1 %collective-permute-done.15.refs_5_ = bf16[128,2048]{1,0:T(8,128)(2,1)} collective-permute-done((bf16[128,2048]{1,0:T(8,128)(2,1)}, bf16[128,2048]{1,0:T(8,128)(2,1)}, u32[]{:S(2)}, u32[]{:S(2)}) %collective-permute-start.15) | collective-permute-done | bytes 524320 | tf_op jit(solution)/shard_map/ppermute | solution.py:31
  97.9 3.0 %partials.11 = (bf16[256,1024]{1,0:T(8,128)(2,1)S(1)}, bf16[256,1024]{1,0:T(8,128)(2,1)S(1)}) custom-call(s32[1]{0:T(128)} %bitcast.z_ref, bf16[1024,1024]{1,0:T(8,128)(2,1)S(1)} %dynamic-slice_dynamic-update-slice_fusion.cot_ref, bf16[128,2048]{1,0:T(8,128)(2,1)} %copy-done, bf16[128,2048]{1,0:T(8,128)(2,1)} %collective-permute-done.2.refs_1_, ...), custom_call_target="tpu_custom_call" | custom-call | tf_op jit(solution)/shard_map/partials/pallas_call | solution.py:94
  101.0 1.3 collective-permute-start.22
  102.5 3.8 %partials.6 = (bf16[256,1280]{1,0:T(8,128)(2,1)S(1)}, f32[256,1280]{1,0:T(8,128)S(1)}) custom-call(s32[1]{0:T(128)} %bitcast.z_ref, bf16[1024,1024]{1,0:T(8,128)(2,1)S(1)} %dynamic-slice_dynamic-update-slice_fusion.cot_ref, bf16[128,1280]{1,0:T(8,128)(2,1)} %copy-done.4, bf16[128,1280]{1,0:T(8,128)(2,1)} %copy-done.7, bf16[128,1280]{1,0:T(8,128)(2,1)} %copy-done.8, ...), custom_call_target="tpu_custom_call" | custom-call | tf_op jit(solution)/shard_map/partials/pallas_call | solution.py:94
  106.3 1.2 add_convert_fusion.1
  107.7 2.7 %collective-permute-start.12 = (bf16[128,1280]{1,0:T(8,128)(2,1)S(1)}, bf16[128,1280]{1,0:T(8,128)(2,1)S(1)}, u32[]{:S(2)}, u32[]{:S(2)}) collective-permute-start(bf16[128,1280]{1,0:T(8,128)(2,1)S(1)} %get-tuple-element.43), channel_id=1, source_target_pairs={{0,24},{8,0},{16,8},{24,16},{1,25},{9,1},{17,9},{25,17},{2,26},{10... | collective-permute-start | bytes 983048 | tf_op jit(solution)/shard_map/ppermute | solution.py:31
  110.9 3.0 %partials.9 = (bf16[256,1024]{1,0:T(8,128)(2,1)S(1)}, bf16[256,1024]{1,0:T(8,128)(2,1)S(1)}) custom-call(s32[1]{0:T(128)} %bitcast.z_ref, bf16[1024,1024]{1,0:T(8,128)(2,1)S(1)} %dynamic-slice_dynamic-update-slice_fusion.cot_ref, bf16[128,2048]{1,0:T(8,128)(2,1)} %copy-done, bf16[128,2048]{1,0:T(8,128)(2,1)} %collective-permute-done.2.refs_1_, ...), custom_call_target="tpu_custom_call" | custom-call | tf_op jit(solution)/shard_map/partials/pallas_call | solution.py:94
  113.9 1.6 %collective-permute-start.18 = (bf16[256,1024]{1,0:T(8,128)(2,1)S(1)}, bf16[256,1024]{1,0:T(8,128)(2,1)S(1)}, u32[]{:S(2)}, u32[]{:S(2)}) collective-permute-start(bf16[256,1024]{1,0:T(8,128)(2,1)S(1)} %get-tuple-element.21), channel_id=1, source_target_pairs={{0,24},{8,0},{16,8},{24,16},{1,25},{9,1},{17,9},{25,17},{2,26},{10... | collective-permute-start | bytes 1572872 | tf_op jit(solution)/shard_map/ppermute | solution.py:31
  115.5 3.0 %partials.10 = (bf16[256,1024]{1,0:T(8,128)(2,1)S(1)}, f32[256,1024]{1,0:T(8,128)S(1)}) custom-call(s32[1]{0:T(128)} %bitcast.z_ref, bf16[1024,1024]{1,0:T(8,128)(2,1)S(1)} %dynamic-slice_dynamic-update-slice_fusion.cot_ref, bf16[128,2048]{1,0:T(8,128)(2,1)} %copy-done, bf16[128,2048]{1,0:T(8,128)(2,1)} %collective-permute-done.2.refs_1_, ...), custom_call_target="tpu_custom_call" | custom-call | tf_op jit(solution)/shard_map/partials/pallas_call | solution.py:94
  118.6 3.1 %partials.8 = (bf16[256,1024]{1,0:T(8,128)(2,1)S(1)}, f32[256,1024]{1,0:T(8,128)S(1)}) custom-call(s32[1]{0:T(128)} %bitcast.z_ref, bf16[1024,1024]{1,0:T(8,128)(2,1)S(1)} %dynamic-slice_dynamic-update-slice_fusion.cot_ref, bf16[128,2048]{1,0:T(8,128)(2,1)} %copy-done, bf16[128,2048]{1,0:T(8,128)(2,1)} %collective-permute-done.2.refs_1_, ...), custom_call_target="tpu_custom_call" | custom-call | tf_op jit(solution)/shard_map/partials/pallas_call | solution.py:94
  122.3 1.3 slice.148
  123.6 1.0 slice.149
  124.6 2.6 %collective-permute-start.25 = (bf16[128,1024]{1,0:T(8,128)(2,1)S(1)}, bf16[128,1024]{1,0:T(8,128)(2,1)S(1)}, u32[]{:S(2)}, u32[]{:S(2)}) collective-permute-start(bf16[128,1024]{1,0:T(8,128)(2,1)S(1)} %get-tuple-element.45), channel_id=1, source_target_pairs={{0,24},{8,0},{16,8},{24,16},{1,25},{9,1},{17,9},{25,17},{2,26},{10... | collective-permute-start | bytes 786440 | tf_op jit(solution)/shard_map/ppermute | solution.py:31
  127.5 1.1 subtract_convert_fusion.3
  128.6 7.8 %collective-permute-start.26 = (bf16[256,256]{1,0:T(8,128)(2,1)S(1)}, bf16[256,256]{1,0:T(8,128)(2,1)S(1)}, u32[]{:S(2)}, u32[]{:S(2)}) collective-permute-start(bf16[256,256]{1,0:T(8,128)(2,1)S(1)} %slice.162), channel_id=1, source_target_pairs={{0,1},{1,2},{2,3},{3,4},{4,5},{5,6},{6,7},{8,9},{9,10},{10,11},{11... | collective-permute-start | bytes 393224 | tf_op jit(solution)/shard_map/ppermute | solution.py:188
  136.4 2.0 %collective-permute-start.27 = (bf16[256,256]{1,0:T(8,128)(2,1)S(1)}, bf16[256,256]{1,0:T(8,128)(2,1)S(1)}, u32[]{:S(2)}, u32[]{:S(2)}) collective-permute-start(bf16[256,256]{1,0:T(8,128)(2,1)S(1)} %slice.163), channel_id=1, source_target_pairs={{1,0},{2,1},{3,2},{4,3},{5,4},{6,5},{7,6},{9,8},{10,9},{11,10},{12... | collective-permute-start | bytes 393224 | tf_op jit(solution)/shard_map/ppermute | solution.py:189
  139.3 2.5 %collective-permute-start.21 = (bf16[128,1024]{1,0:T(8,128)(2,1)S(1)}, bf16[128,1024]{1,0:T(8,128)(2,1)S(1)}, u32[]{:S(2)}, u32[]{:S(2)}) collective-permute-start(bf16[128,1024]{1,0:T(8,128)(2,1)S(1)} %get-tuple-element.47), channel_id=1, source_target_pairs={{0,24},{8,0},{16,8},{24,16},{1,25},{9,1},{17,9},{25,17},{2,26},{10... | collective-permute-start | bytes 786440 | tf_op jit(solution)/shard_map/ppermute | solution.py:31
  141.9 0.8 collective-permute-done.27
  142.8 3.2 %collective-permute-done.20 = bf16[128,1024]{1,0:T(8,128)(2,1)S(1)} collective-permute-done((bf16[128,1024]{1,0:T(8,128)(2,1)S(1)}, bf16[128,1024]{1,0:T(8,128)(2,1)S(1)}, u32[]{:S(2)}, u32[]{:S(2)}) %collective-permute-start.20) | collective-permute-done | bytes 262176 | tf_op jit(solution)/shard_map/ppermute | solution.py:31
  146.1 1.0 fusion.24
  147.2 0.8 slice-done
  148.2 1.0 fusion.25
  149.3 2.4 %dynamic-slice_select_fusion = bf16[256,3840]{1,0:T(8,128)(2,1)} fusion(bf16[256,4352]{1,0:T(8,128)(2,1)S(1)} %get-tuple-element.30, s32[]{:T(128)S(6)} %select_n.79, pred[3840]{0:T(1024)(128)(4,1)S(1)} %iota_compare_fusion), kind=kLoop, calls=%fused_computation | loop fusion | flops 983040 | bytes 3936004 | tf_op jit(solution)/shard_map/jit(_where)/select_n | solution.py:205
  (94 shorter events, 4.4 us)
Async XLA Ops:
  1.7 32.5 %copy-start = (bf16[128,2048]{1,0:T(8,128)(2,1)}, bf16[128,2048]{1,0:T(8,128)(2,1)S(1)}, u32[]{:S(2)}) copy-start(bf16[128,2048]{1,0:T(8,128)(2,1)S(1)} %slice.114.refs_0_) | copy-start | bytes 1572868
  1.7 30.8 %collective-permute-start.2 = (bf16[128,2048]{1,0:T(8,128)(2,1)S(1)}, bf16[128,2048]{1,0:T(8,128)(2,1)}, u32[]{:S(2)}, u32[]{:S(2)}) collective-permute-start(bf16[128,2048]{1,0:T(8,128)(2,1)S(1)} %slice.114.refs_0_), channel_id=1, source_target_pairs={{0,32},{32,64},{64,96},{96,128},{128,160},{160,192},{192,224},{224... | collective-permute-start | bytes 1572872 | tf_op jit(solution)/shard_map/ppermute | solution.py:31
  4.3 28.3 %collective-permute-start.3 = (bf16[128,2048]{1,0:T(8,128)(2,1)S(1)}, bf16[128,2048]{1,0:T(8,128)(2,1)S(1)}, u32[]{:S(2)}, u32[]{:S(2)}) collective-permute-start(bf16[128,2048]{1,0:T(8,128)(2,1)S(1)} %slice.114.refs_0_), channel_id=1, source_target_pairs={{0,224},{32,0},{64,32},{96,64},{128,96},{160,128},{192,160},{224,1... | collective-permute-start | bytes 1572872 | tf_op jit(solution)/shard_map/ppermute | solution.py:31
  10.0 22.5 %all-to-all-start = ((bf16[16,8,1024]{2,0,1:T(8,128)(2,1)}), bf16[16,8,1024]{2,0,1:T(8,128)(2,1)S(1)}, u32[]{:S(2)}, u32[]{:S(2)}) async-start(bf16[16,8,1024]{2,0,1:T(8,128)(2,1)} %bitcast.13), calls=%async_computation | async-start | bytes 524288 | tf_op jit(solution)/shard_map/all_to_all | solution.py:150
  16.2 1.6 %copy-start.4 = (bf16[128,1280]{1,0:T(8,128)(2,1)}, bf16[128,1280]{1,0:T(8,128)(2,1)S(1)}, u32[]{:S(2)}) copy-start(bf16[128,1280]{1,0:T(8,128)(2,1)S(1)} %pad_maximum_fusion.refs_0_) | copy-start | bytes 983044
  16.2 16.3 %collective-permute-start = (bf16[128,1280]{1,0:T(8,128)(2,1)S(1)}, bf16[128,1280]{1,0:T(8,128)(2,1)S(1)}, u32[]{:S(2)}, u32[]{:S(2)}) collective-permute-start(bf16[128,1280]{1,0:T(8,128)(2,1)S(1)} %pad_maximum_fusion.refs_0_), channel_id=1, source_target_pairs={{0,32},{32,64},{64,96},{96,128},{128,160},{160,192},{192,224},{224... | collective-permute-start | bytes 983048 | tf_op jit(solution)/shard_map/ppermute | solution.py:31
  17.8 14.7 %collective-permute-start.1 = (bf16[128,1280]{1,0:T(8,128)(2,1)S(1)}, bf16[128,1280]{1,0:T(8,128)(2,1)S(1)}, u32[]{:S(2)}, u32[]{:S(2)}) collective-permute-start(bf16[128,1280]{1,0:T(8,128)(2,1)S(1)} %pad_maximum_fusion.refs_0_), channel_id=1, source_target_pairs={{0,224},{32,0},{64,32},{96,64},{128,96},{160,128},{192,160},{224,1... | collective-permute-start | bytes 983048 | tf_op jit(solution)/shard_map/ppermute | solution.py:31
  32.5 7.2 %copy-start.7 = (bf16[128,1280]{1,0:T(8,128)(2,1)}, bf16[128,1280]{1,0:T(8,128)(2,1)S(1)}, u32[]{:S(2)}) copy-start(bf16[128,1280]{1,0:T(8,128)(2,1)S(1)} %collective-permute-done.refs_1_) | copy-start | bytes 983044
  32.5 10.0 %copy-start.8 = (bf16[128,1280]{1,0:T(8,128)(2,1)}, bf16[128,1280]{1,0:T(8,128)(2,1)S(1)}, u32[]{:S(2)}) copy-start(bf16[128,1280]{1,0:T(8,128)(2,1)S(1)} %collective-permute-done.1.refs_2_) | copy-start | bytes 983044
  32.5 7.2 %copy-start.1 = (bf16[128,2048]{1,0:T(8,128)(2,1)}, bf16[128,2048]{1,0:T(8,128)(2,1)S(1)}, u32[]{:S(2)}) copy-start(bf16[128,2048]{1,0:T(8,128)(2,1)S(1)} %collective-permute-done.3.refs_2_) | copy-start | bytes 1572868
  34.2 32.6 %all-to-all-start.1 = ((bf16[8,128,1024]{2,1,0:T(8,128)(2,1)}), bf16[8,128,1024]{2,1,0:T(8,128)(2,1)S(1)}, u32[]{:S(2)}, u32[]{:S(2)}) async-start(bf16[8,128,1024]{2,1,0:T(8,128)(2,1)} %broadcast_in_dim.26), calls=%async_computation.1 | async-start | bytes 4194304 | tf_op jit(solution)/shard_map/all_to_all | solution.py:53
  39.7 10.6 %collective-permute-start.4 = (bf16[128,1280]{1,0:T(8,128)(2,1)S(1)}, bf16[128,1280]{1,0:T(8,128)(2,1)}, u32[]{:S(2)}, u32[]{:S(2)}) collective-permute-start(bf16[128,1280]{1,0:T(8,128)(2,1)S(1)} %collective-permute-done.refs_1_), channel_id=1, source_target_pairs={{0,32},{32,64},{64,96},{96,128},{128,160},{160,192},{192,224},{224... | collective-permute-start | bytes 983048 | tf_op jit(solution)/shard_map/ppermute | solution.py:31
  39.8 24.3 %collective-permute-start.14 = (bf16[128,2048]{1,0:T(8,128)(2,1)S(1)}, bf16[128,2048]{1,0:T(8,128)(2,1)}, u32[]{:S(2)}, u32[]{:S(2)}) collective-permute-start(bf16[128,2048]{1,0:T(8,128)(2,1)S(1)} %collective-permute-done.3.refs_2_), channel_id=1, source_target_pairs={{0,224},{32,0},{64,32},{96,64},{128,96},{160,128},{192,160},{224,1... | collective-permute-start | bytes 1572872 | tf_op jit(solution)/shard_map/ppermute | solution.py:31
  42.5 18.5 %collective-permute-start.5 = (bf16[128,1280]{1,0:T(8,128)(2,1)S(1)}, bf16[128,1280]{1,0:T(8,128)(2,1)}, u32[]{:S(2)}, u32[]{:S(2)}) collective-permute-start(bf16[128,1280]{1,0:T(8,128)(2,1)S(1)} %collective-permute-done.1.refs_2_), channel_id=1, source_target_pairs={{0,224},{32,0},{64,32},{96,64},{128,96},{160,128},{192,160},{224,1... | collective-permute-start | bytes 983048 | tf_op jit(solution)/shard_map/ppermute | solution.py:31
  50.3 13.8 %collective-permute-start.6 = (bf16[128,1280]{1,0:T(8,128)(2,1)}, bf16[128,1280]{1,0:T(8,128)(2,1)S(1)}, u32[]{:S(2)}, u32[]{:S(2)}) collective-permute-start(bf16[128,1280]{1,0:T(8,128)(2,1)} %collective-permute-done.4.refs_3_), channel_id=1, source_target_pairs={{0,32},{32,64},{64,96},{96,128},{128,160},{160,192},{192,224},{224... | collective-permute-start | bytes 983048 | tf_op jit(solution)/shard_map/ppermute | solution.py:31
  50.3 34.8 %collective-permute-start.13 = (bf16[128,2048]{1,0:T(8,128)(2,1)}, bf16[128,2048]{1,0:T(8,128)(2,1)}, u32[]{:S(2)}, u32[]{:S(2)}) collective-permute-start(bf16[128,2048]{1,0:T(8,128)(2,1)} %collective-permute-done.2.refs_1_), channel_id=1, source_target_pairs={{0,32},{32,64},{64,96},{96,128},{128,160},{160,192},{192,224},{224... | collective-permute-start | bytes 1572872 | tf_op jit(solution)/shard_map/ppermute | solution.py:31
  61.0 10.2 %collective-permute-start.7 = (bf16[128,1280]{1,0:T(8,128)(2,1)}, bf16[128,1280]{1,0:T(8,128)(2,1)S(1)}, u32[]{:S(2)}, u32[]{:S(2)}) collective-permute-start(bf16[128,1280]{1,0:T(8,128)(2,1)} %collective-permute-done.5.refs_4_), channel_id=1, source_target_pairs={{0,224},{32,0},{64,32},{96,64},{128,96},{160,128},{192,160},{224,1... | collective-permute-start | bytes 983048 | tf_op jit(solution)/shard_map/ppermute | solution.py:31
  64.1 2.9 %copy-start.9 = (bf16[128,1280]{1,0:T(8,128)(2,1)}, bf16[128,1280]{1,0:T(8,128)(2,1)S(1)}, u32[]{:S(2)}) copy-start(bf16[128,1280]{1,0:T(8,128)(2,1)S(1)} %collective-permute-done.6.refs_5_) | copy-start | bytes 983044
  64.1 14.4 %collective-permute-start.8 = (bf16[128,1280]{1,0:T(8,128)(2,1)S(1)}, bf16[128,1280]{1,0:T(8,128)(2,1)}, u32[]{:S(2)}, u32[]{:S(2)}) collective-permute-start(bf16[128,1280]{1,0:T(8,128)(2,1)S(1)} %collective-permute-done.6.refs_5_), channel_id=1, source_target_pairs={{0,32},{32,64},{64,96},{96,128},{128,160},{160,192},{192,224},{224... | collective-permute-start | bytes 983048 | tf_op jit(solution)/shard_map/ppermute | solution.py:31
  64.1 21.1 %collective-permute-start.16 = (bf16[128,2048]{1,0:T(8,128)(2,1)}, bf16[128,2048]{1,0:T(8,128)(2,1)}, u32[]{:S(2)}, u32[]{:S(2)}) collective-permute-start(bf16[128,2048]{1,0:T(8,128)(2,1)} %collective-permute-done.14.refs_4_), channel_id=1, source_target_pairs={{0,224},{32,0},{64,32},{96,64},{128,96},{160,128},{192,160},{224,1... | collective-permute-start | bytes 1572872 | tf_op jit(solution)/shard_map/ppermute | solution.py:31
  71.2 7.3 %copy-start.10 = (bf16[128,1280]{1,0:T(8,128)(2,1)}, bf16[128,1280]{1,0:T(8,128)(2,1)S(1)}, u32[]{:S(2)}) copy-start(bf16[128,1280]{1,0:T(8,128)(2,1)S(1)} %collective-permute-done.7.refs_6_) | copy-start | bytes 983044
  78.5 10.1 %copy-start.15 = (s32[8]{0:T(128)S(1)}, s32[8]{0:T(128)}, u32[]{:S(2)}) copy-start(s32[8]{0:T(128)} %param.12) | copy-start | bytes 100
  82.3 24.1 %collective-permute-start.10 = (bf16[256,1280]{1,0:T(8,128)(2,1)S(1)}, bf16[256,1280]{1,0:T(8,128)(2,1)}, u32[]{:S(2)}, u32[]{:S(2)}) collective-permute-start(bf16[256,1280]{1,0:T(8,128)(2,1)S(1)} %get-tuple-element.18), channel_id=1, source_target_pairs={{0,8},{8,16},{16,24},{24,0},{1,9},{9,17},{17,25},{25,1},{2,10},{10... | collective-permute-start | bytes 1966088 | tf_op jit(solution)/shard_map/ppermute | solution.py:31
  83.6 22.7 %collective-permute-start.9 = (bf16[256,1280]{1,0:T(8,128)(2,1)S(1)}, bf16[256,1280]{1,0:T(8,128)(2,1)}, u32[]{:S(2)}, u32[]{:S(2)}) collective-permute-start(bf16[256,1280]{1,0:T(8,128)(2,1)S(1)} %get-tuple-element.17), channel_id=1, source_target_pairs={{0,24},{8,0},{16,8},{24,16},{1,25},{9,1},{17,9},{25,17},{2,26},{10... | collective-permute-start | bytes 1966088 | tf_op jit(solution)/shard_map/ppermute | solution.py:31
  85.2 12.8 %collective-permute-start.15 = (bf16[128,2048]{1,0:T(8,128)(2,1)}, bf16[128,2048]{1,0:T(8,128)(2,1)}, u32[]{:S(2)}, u32[]{:S(2)}) collective-permute-start(bf16[128,2048]{1,0:T(8,128)(2,1)} %collective-permute-done.13.refs_3_), channel_id=1, source_target_pairs={{0,32},{32,64},{64,96},{96,128},{128,160},{160,192},{192,224},{224... | collective-permute-start | bytes 1572872 | tf_op jit(solution)/shard_map/ppermute | solution.py:31
  85.2 12.8 %collective-permute-start.17 = (bf16[128,2048]{1,0:T(8,128)(2,1)}, bf16[128,2048]{1,0:T(8,128)(2,1)}, u32[]{:S(2)}, u32[]{:S(2)}) collective-permute-start(bf16[128,2048]{1,0:T(8,128)(2,1)} %collective-permute-done.16.refs_6_), channel_id=1, source_target_pairs={{0,224},{32,0},{64,32},{96,64},{128,96},{160,128},{192,160},{224,1... | collective-permute-start | bytes 1572872 | tf_op jit(solution)/shard_map/ppermute | solution.py:31
  101.0 20.6 %collective-permute-start.22 = (bf16[256,1024]{1,0:T(8,128)(2,1)S(1)}, bf16[256,1024]{1,0:T(8,128)(2,1)S(1)}, u32[]{:S(2)}, u32[]{:S(2)}) collective-permute-start(bf16[256,1024]{1,0:T(8,128)(2,1)S(1)} %get-tuple-element.25), channel_id=1, source_target_pairs={{0,24},{8,0},{16,8},{24,16},{1,25},{9,1},{17,9},{25,17},{2,26},{10... | collective-permute-start | bytes 1572872 | tf_op jit(solution)/shard_map/ppermute | solution.py:31
  102.3 19.6 %collective-permute-start.23 = (bf16[256,1024]{1,0:T(8,128)(2,1)S(1)}, bf16[256,1024]{1,0:T(8,128)(2,1)S(1)}, u32[]{:S(2)}, u32[]{:S(2)}) collective-permute-start(bf16[256,1024]{1,0:T(8,128)(2,1)S(1)} %get-tuple-element.26), channel_id=1, source_target_pairs={{0,8},{8,16},{16,24},{24,0},{1,9},{9,17},{17,25},{25,1},{2,10},{10... | collective-permute-start | bytes 1572872 | tf_op jit(solution)/shard_map/ppermute | solution.py:31
  107.6 17.0 %collective-permute-start.11 = (bf16[128,1280]{1,0:T(8,128)(2,1)S(1)}, bf16[128,1280]{1,0:T(8,128)(2,1)S(1)}, u32[]{:S(2)}, u32[]{:S(2)}) collective-permute-start(bf16[128,1280]{1,0:T(8,128)(2,1)S(1)} %get-tuple-element.42), channel_id=1, source_target_pairs={{0,8},{8,16},{16,24},{24,0},{1,9},{9,17},{17,25},{25,1},{2,10},{10... | collective-permute-start | bytes 983048 | tf_op jit(solution)/shard_map/ppermute | solution.py:31
  107.7 19.5 %collective-permute-start.12 = (bf16[128,1280]{1,0:T(8,128)(2,1)S(1)}, bf16[128,1280]{1,0:T(8,128)(2,1)S(1)}, u32[]{:S(2)}, u32[]{:S(2)}) collective-permute-start(bf16[128,1280]{1,0:T(8,128)(2,1)S(1)} %get-tuple-element.43), channel_id=1, source_target_pairs={{0,24},{8,0},{16,8},{24,16},{1,25},{9,1},{17,9},{25,17},{2,26},{10... | collective-permute-start | bytes 983048 | tf_op jit(solution)/shard_map/ppermute | solution.py:31
  113.9 22.4 %collective-permute-start.18 = (bf16[256,1024]{1,0:T(8,128)(2,1)S(1)}, bf16[256,1024]{1,0:T(8,128)(2,1)S(1)}, u32[]{:S(2)}, u32[]{:S(2)}) collective-permute-start(bf16[256,1024]{1,0:T(8,128)(2,1)S(1)} %get-tuple-element.21), channel_id=1, source_target_pairs={{0,24},{8,0},{16,8},{24,16},{1,25},{9,1},{17,9},{25,17},{2,26},{10... | collective-permute-start | bytes 1572872 | tf_op jit(solution)/shard_map/ppermute | solution.py:31
  121.6 17.1 %copy-start.11 = (bf16[256,1024]{1,0:T(8,128)(2,1)}, bf16[256,1024]{1,0:T(8,128)(2,1)S(1)}, u32[]{:S(2)}) copy-start(bf16[256,1024]{1,0:T(8,128)(2,1)S(1)} %collective-permute-done.22) | copy-start | bytes 1572868
  121.6 16.7 %collective-permute-start.19 = (bf16[256,1024]{1,0:T(8,128)(2,1)S(1)}, bf16[256,1024]{1,0:T(8,128)(2,1)S(1)}, u32[]{:S(2)}, u32[]{:S(2)}) collective-permute-start(bf16[256,1024]{1,0:T(8,128)(2,1)S(1)} %get-tuple-element.22), channel_id=1, source_target_pairs={{0,8},{8,16},{16,24},{24,0},{1,9},{9,17},{17,25},{25,1},{2,10},{10... | collective-permute-start | bytes 1572872 | tf_op jit(solution)/shard_map/ppermute | solution.py:31
  121.9 16.8 %copy-start.12 = (bf16[256,1024]{1,0:T(8,128)(2,1)}, bf16[256,1024]{1,0:T(8,128)(2,1)S(1)}, u32[]{:S(2)}) copy-start(bf16[256,1024]{1,0:T(8,128)(2,1)S(1)} %collective-permute-done.23) | copy-start | bytes 1572868
  121.9 5.5 %copy-start.6 = (bf16[256,3328]{1,0:T(8,128)(2,1)S(1)}, bf16[256,3328]{1,0:T(8,128)(2,1)}, u32[]{:S(2)}) copy-start(bf16[256,3328]{1,0:T(8,128)(2,1)} %param.10) | copy-start | bytes 5111812
  122.1 25.1 %collective-permute-start.24 = (bf16[128,1024]{1,0:T(8,128)(2,1)S(1)}, bf16[128,1024]{1,0:T(8,128)(2,1)S(1)}, u32[]{:S(2)}, u32[]{:S(2)}) collective-permute-start(bf16[128,1024]{1,0:T(8,128)(2,1)S(1)} %get-tuple-element.44), channel_id=1, source_target_pairs={{0,8},{8,16},{16,24},{24,0},{1,9},{9,17},{17,25},{25,1},{2,10},{10... | collective-permute-start | bytes 786440 | tf_op jit(solution)/shard_map/ppermute | solution.py:31
  122.3 5.2 %copy-start.5 = (bf16[256,3328]{1,0:T(8,128)(2,1)S(1)}, bf16[256,3328]{1,0:T(8,128)(2,1)}, u32[]{:S(2)}) copy-start(bf16[256,3328]{1,0:T(8,128)(2,1)} %param.11) | copy-start | bytes 5111812
  124.6 2.9 %copy-start.3 = (f32[256,3328]{1,0:T(8,128)S(1)}, f32[256,3328]{1,0:T(8,128)}, u32[]{:S(2)}) copy-start(f32[256,3328]{1,0:T(8,128)} %param.9) | copy-start | bytes 10223620
  124.6 22.6 %collective-permute-start.25 = (bf16[128,1024]{1,0:T(8,128)(2,1)S(1)}, bf16[128,1024]{1,0:T(8,128)(2,1)S(1)}, u32[]{:S(2)}, u32[]{:S(2)}) collective-permute-start(bf16[128,1024]{1,0:T(8,128)(2,1)S(1)} %get-tuple-element.45), channel_id=1, source_target_pairs={{0,24},{8,0},{16,8},{24,16},{1,25},{9,1},{17,9},{25,17},{2,26},{10... | collective-permute-start | bytes 786440 | tf_op jit(solution)/shard_map/ppermute | solution.py:31
  128.6 10.7 %collective-permute-start.26 = (bf16[256,256]{1,0:T(8,128)(2,1)S(1)}, bf16[256,256]{1,0:T(8,128)(2,1)S(1)}, u32[]{:S(2)}, u32[]{:S(2)}) collective-permute-start(bf16[256,256]{1,0:T(8,128)(2,1)S(1)} %slice.162), channel_id=1, source_target_pairs={{0,1},{1,2},{2,3},{3,4},{4,5},{5,6},{6,7},{8,9},{9,10},{10,11},{11... | collective-permute-start | bytes 393224 | tf_op jit(solution)/shard_map/ppermute | solution.py:188
  136.4 2.5 %copy-start.13 = (bf16[256,1024]{1,0:T(8,128)(2,1)}, bf16[256,1024]{1,0:T(8,128)(2,1)S(1)}, u32[]{:S(2)}) copy-start(bf16[256,1024]{1,0:T(8,128)(2,1)S(1)} %collective-permute-done.18) | copy-start | bytes 1572868
  136.4 6.3 %collective-permute-start.27 = (bf16[256,256]{1,0:T(8,128)(2,1)S(1)}, bf16[256,256]{1,0:T(8,128)(2,1)S(1)}, u32[]{:S(2)}, u32[]{:S(2)}) collective-permute-start(bf16[256,256]{1,0:T(8,128)(2,1)S(1)} %slice.163), channel_id=1, source_target_pairs={{1,0},{2,1},{3,2},{4,3},{5,4},{6,5},{7,6},{9,8},{10,9},{11,10},{12... | collective-permute-start | bytes 393224 | tf_op jit(solution)/shard_map/ppermute | solution.py:189
  138.6 7.4 %collective-permute-start.20 = (bf16[128,1024]{1,0:T(8,128)(2,1)S(1)}, bf16[128,1024]{1,0:T(8,128)(2,1)S(1)}, u32[]{:S(2)}, u32[]{:S(2)}) collective-permute-start(bf16[128,1024]{1,0:T(8,128)(2,1)S(1)} %get-tuple-element.46), channel_id=1, source_target_pairs={{0,8},{8,16},{16,24},{24,0},{1,9},{9,17},{17,25},{25,1},{2,10},{10... | collective-permute-start | bytes 786440 | tf_op jit(solution)/shard_map/ppermute | solution.py:31
  139.2 6.9 %slice-start.2 = ((bf16[256,1024]{1,0:T(8,128)(2,1)}), bf16[128,1024]{1,0:T(8,128)(2,1)S(1)}, s32[]{:S(2)}) async-start(bf16[256,1024]{1,0:T(8,128)(2,1)} %copy-done.13), calls=%async_computation.4 | async-start | bytes 524288 | tf_op jit(solution)/shard_map/slice | solution.py:125
  139.2 6.9 %slice-start.3 = ((bf16[256,1024]{1,0:T(8,128)(2,1)}), bf16[128,1024]{1,0:T(8,128)(2,1)S(1)}, s32[]{:S(2)}) async-start(bf16[256,1024]{1,0:T(8,128)(2,1)} %copy-done.14), calls=%async_computation.5 | async-start | bytes 524288 | tf_op jit(solution)/shard_map/slice | solution.py:125
  139.3 6.8 %collective-permute-start.21 = (bf16[128,1024]{1,0:T(8,128)(2,1)S(1)}, bf16[128,1024]{1,0:T(8,128)(2,1)S(1)}, u32[]{:S(2)}, u32[]{:S(2)}) collective-permute-start(bf16[128,1024]{1,0:T(8,128)(2,1)S(1)} %get-tuple-element.47), channel_id=1, source_target_pairs={{0,24},{8,0},{16,8},{24,16},{1,25},{9,1},{17,9},{25,17},{2,26},{10... | collective-permute-start | bytes 786440 | tf_op jit(solution)/shard_map/ppermute | solution.py:31
  147.1 1.0 slice-start.1
  149.2 2.4 %copy-start.2 = (f32[256,3328]{1,0:T(8,128)}, f32[256,3328]{1,0:T(8,128)S(1)}, u32[]{:S(2)}) copy-start(f32[256,3328]{1,0:T(8,128)S(1)} %constant_dynamic-update-slice_fusion.3) | copy-start | bytes 10223620
  (2 other events, 1.7 us)

commit v4 on v3

--- a/solution.py
+++ b/solution.py
@@ -131,7 +131,7 @@
     first_new = beta_first * first_moment + (1.0 - beta_first) * gradient
     second_new = beta_second * second_moment + (1.0 - beta_second) * gradient * gradient
     update = (
-        first_new / first_fix / (jnp.sqrt(second_new / second_fix) + epsilon) + decay_rate * master
+        first_new * first_fix / (jnp.sqrt(second_new * second_fix) + epsilon) + decay_rate * master
     )
     master_new = master - learn_rate * update
     return (master_new, update)
@@ -154,8 +154,8 @@
     cotangent = cotangent_of(mine, out_grad.shape[0])
 
     steps_done = step_count[0].astype(jnp.float32)
-    first_fix = 1.0 - jnp.power(beta_first, steps_done)
-    second_fix = 1.0 - jnp.power(beta_second, steps_done)
+    first_fix = 1.0 / (1.0 - jnp.power(beta_first, steps_done))
+    second_fix = 1.0 / (1.0 - jnp.power(beta_second, steps_done))
 
     rim_gradient = ring_scatter(
         partials(z, cotangent, rim_pieces, 0, rim.shape[1], rim.shape[1] // 2)

time: 154 us -> 154 us (level)
  no operation moved by 1% of the time
where the time goes in v4:
time: 154 us; the launch traced here: 152 us
  starting transfers between devices  58.6 us (38%)
  waiting for transfers between devices  51.3 us (33%)
  Pallas kernels  19.7 us (13%)
  local copies, waits for them, and re-layouts  10.8 us (7%)
  other arithmetic  8.58 us (6%)
  between operations  2.65 us (2%)
    ppermute x26, waiting for transfers between devices, shift(): lax.ppermute(value, axis, [(i, (i + by) % count) for i in range(count)])  50.5 us
    ppermute x26, starting transfers between devices, shift(): lax.ppermute(value, axis, [(i, (i + by) % count) for i in range(count)])  38.1 us
    pallas_call x6, Pallas kernels, half_partials(): pl.pallas_call(body, grid=(cols // tile,), in_specs=[pl.BlockSpec(memory_...  19.7 us
    ppermute x1, starting transfers between devices, per_device(): left = lax.ppermute(tail, TENSOR, [(i, i + 1) for i in range(last)])  7.76 us
    all_to_all x1, starting transfers between devices, cotangent_of(): lax.all_to_all(copies, TENSOR, split_axis=0, concat_axis=0, tiled=True)  5.52 us
    all_to_all x1, starting transfers between devices, per_device(): lax.all_to_all(out_grad, 'z', split_axis=1, concat_axis=0, tiled=True)  5.2 us
    slice x10, local copies, waits for them, and re-layouts, ring_scatter(): direct = jnp.concatenate([above[half:], below[half:]], axis=0).astype(wide)  3.26 us
  transfers between devices with their start and end apart: 30, of which 9 were waited for; matrix products, arithmetic and copies ran while one was open for 8% of the time, Pallas kernels for 13%

profile of v4, /device:TPU:1, one launch (start us, length us, event | category | flops | bytes accessed | tf_op | source)
XLA Modules:
  0.0 151.6 jit_solution(11835560365364357165)
XLA Ops:
  0.6 1.1 slice.114.refs_0_
  1.7 2.5 %collective-permute-start.2 = (bf16[128,2048]{1,0:T(8,128)(2,1)S(1)}, bf16[128,2048]{1,0:T(8,128)(2,1)}, u32[]{:S(2)}, u32[]{:S(2)}) collective-permute-start(bf16[128,2048]{1,0:T(8,128)(2,1)S(1)} %slice.114.refs_0_), channel_id=1, source_target_pairs={{0,32},{32,64},{64,96},{96,128},{128,160},{160,192},{192,224},{224... | collective-permute-start | bytes 1572872 | tf_op jit(solution)/shard_map/ppermute | solution.py:31
  4.3 4.0 %collective-permute-start.3 = (bf16[128,2048]{1,0:T(8,128)(2,1)S(1)}, bf16[128,2048]{1,0:T(8,128)(2,1)S(1)}, u32[]{:S(2)}, u32[]{:S(2)}) collective-permute-start(bf16[128,2048]{1,0:T(8,128)(2,1)S(1)} %slice.114.refs_0_), channel_id=1, source_target_pairs={{0,224},{32,0},{64,32},{96,64},{128,96},{160,128},{192,160},{224,1... | collective-permute-start | bytes 1572872 | tf_op jit(solution)/shard_map/ppermute | solution.py:31
  8.3 1.7 %copy.16 = bf16[2,8,8,1024]{3,2,0,1:T(8,128)(2,1)} copy(bf16[2,8,8,1024]{3,2,1,0:T(8,128)(2,1)} %bitcast.24) | data formatting | bytes 524288 | tf_op jit(solution)/shard_map/all_to_all | solution.py:150
  10.0 5.2 %all-to-all-start = ((bf16[16,8,1024]{2,0,1:T(8,128)(2,1)}), bf16[16,8,1024]{2,0,1:T(8,128)(2,1)S(1)}, u32[]{:S(2)}, u32[]{:S(2)}) async-start(bf16[16,8,1024]{2,0,1:T(8,128)(2,1)} %bitcast.13), calls=%async_computation | async-start | bytes 524288 | tf_op jit(solution)/shard_map/all_to_all | solution.py:150
  15.2 1.0 fusion.32
  16.2 1.5 %collective-permute-start = (bf16[128,1280]{1,0:T(8,128)(2,1)S(1)}, bf16[128,1280]{1,0:T(8,128)(2,1)S(1)}, u32[]{:S(2)}, u32[]{:S(2)}) collective-permute-start(bf16[128,1280]{1,0:T(8,128)(2,1)S(1)} %pad_maximum_fusion.refs_0_), channel_id=1, source_target_pairs={{0,32},{32,64},{64,96},{96,128},{128,160},{160,192},{192,224},{224... | collective-permute-start | bytes 983048 | tf_op jit(solution)/shard_map/ppermute | solution.py:31
  17.8 1.8 %collective-permute-start.1 = (bf16[128,1280]{1,0:T(8,128)(2,1)S(1)}, bf16[128,1280]{1,0:T(8,128)(2,1)S(1)}, u32[]{:S(2)}, u32[]{:S(2)}) collective-permute-start(bf16[128,1280]{1,0:T(8,128)(2,1)S(1)} %pad_maximum_fusion.refs_0_), channel_id=1, source_target_pairs={{0,224},{32,0},{64,32},{96,64},{128,96},{160,128},{192,160},{224,1... | collective-permute-start | bytes 983048 | tf_op jit(solution)/shard_map/ppermute | solution.py:31
  19.6 12.9 %collective-permute-done.refs_1_ = bf16[128,1280]{1,0:T(8,128)(2,1)S(1)} collective-permute-done((bf16[128,1280]{1,0:T(8,128)(2,1)S(1)}, bf16[128,1280]{1,0:T(8,128)(2,1)S(1)}, u32[]{:S(2)}, u32[]{:S(2)}) %collective-permute-start) | collective-permute-done | bytes 327712 | tf_op jit(solution)/shard_map/ppermute | solution.py:31
  32.5 1.7 %broadcast_in_dim.26 = bf16[8,128,1024]{2,1,0:T(8,128)(2,1)} broadcast(bf16[128,1024]{1,0:T(8,128)(2,1)S(1)} %bitcast.23), dimensions={1,2} | broadcast | bytes 2359296 | tf_op jit(solution)/shard_map/broadcast_in_dim | solution.py:52
  34.2 5.5 %all-to-all-start.1 = ((bf16[8,128,1024]{2,1,0:T(8,128)(2,1)}), bf16[8,128,1024]{2,1,0:T(8,128)(2,1)S(1)}, u32[]{:S(2)}, u32[]{:S(2)}) async-start(bf16[8,128,1024]{2,1,0:T(8,128)(2,1)} %broadcast_in_dim.26), calls=%async_computation.1 | async-start | bytes 4194304 | tf_op jit(solution)/shard_map/all_to_all | solution.py:53
  39.8 2.7 %collective-permute-start.14 = (bf16[128,2048]{1,0:T(8,128)(2,1)S(1)}, bf16[128,2048]{1,0:T(8,128)(2,1)}, u32[]{:S(2)}, u32[]{:S(2)}) collective-permute-start(bf16[128,2048]{1,0:T(8,128)(2,1)S(1)} %collective-permute-done.3.refs_2_), channel_id=1, source_target_pairs={{0,224},{32,0},{64,32},{96,64},{128,96},{160,128},{192,160},{224,1... | collective-permute-start | bytes 1572872 | tf_op jit(solution)/shard_map/ppermute | solution.py:31
  42.5 1.4 collective-permute-start.5
  43.9 6.4 %collective-permute-done.4.refs_3_ = bf16[128,1280]{1,0:T(8,128)(2,1)} collective-permute-done((bf16[128,1280]{1,0:T(8,128)(2,1)S(1)}, bf16[128,1280]{1,0:T(8,128)(2,1)}, u32[]{:S(2)}, u32[]{:S(2)}) %collective-permute-start.4) | collective-permute-done | bytes 327712 | tf_op jit(solution)/shard_map/ppermute | solution.py:31
  50.3 1.2 collective-permute-start.13
  51.6 9.4 %collective-permute-done.5.refs_4_ = bf16[128,1280]{1,0:T(8,128)(2,1)} collective-permute-done((bf16[128,1280]{1,0:T(8,128)(2,1)S(1)}, bf16[128,1280]{1,0:T(8,128)(2,1)}, u32[]{:S(2)}, u32[]{:S(2)}) %collective-permute-start.5) | collective-permute-done | bytes 327712 | tf_op jit(solution)/shard_map/ppermute | solution.py:31
  61.0 3.1 %collective-permute-start.7 = (bf16[128,1280]{1,0:T(8,128)(2,1)}, bf16[128,1280]{1,0:T(8,128)(2,1)S(1)}, u32[]{:S(2)}, u32[]{:S(2)}) collective-permute-start(bf16[128,1280]{1,0:T(8,128)(2,1)} %collective-permute-done.5.refs_4_), channel_id=1, source_target_pairs={{0,224},{32,0},{64,32},{96,64},{128,96},{160,128},{192,160},{224,1... | collective-permute-start | bytes 983048 | tf_op jit(solution)/shard_map/ppermute | solution.py:31
  64.1 2.7 %collective-permute-start.16 = (bf16[128,2048]{1,0:T(8,128)(2,1)}, bf16[128,2048]{1,0:T(8,128)(2,1)}, u32[]{:S(2)}, u32[]{:S(2)}) collective-permute-start(bf16[128,2048]{1,0:T(8,128)(2,1)} %collective-permute-done.14.refs_4_), channel_id=1, source_target_pairs={{0,224},{32,0},{64,32},{96,64},{128,96},{160,128},{192,160},{224,1... | collective-permute-start | bytes 1572872 | tf_op jit(solution)/shard_map/ppermute | solution.py:31
  68.0 3.2 %collective-permute-done.7.refs_6_ = bf16[128,1280]{1,0:T(8,128)(2,1)S(1)} collective-permute-done((bf16[128,1280]{1,0:T(8,128)(2,1)}, bf16[128,1280]{1,0:T(8,128)(2,1)S(1)}, u32[]{:S(2)}, u32[]{:S(2)}) %collective-permute-start.7) | collective-permute-done | bytes 327712 | tf_op jit(solution)/shard_map/ppermute | solution.py:31
  71.2 7.3 %collective-permute-done.8.refs_7_ = bf16[128,1280]{1,0:T(8,128)(2,1)} collective-permute-done((bf16[128,1280]{1,0:T(8,128)(2,1)S(1)}, bf16[128,1280]{1,0:T(8,128)(2,1)}, u32[]{:S(2)}, u32[]{:S(2)}) %collective-permute-start.8) | collective-permute-done | bytes 327712 | tf_op jit(solution)/shard_map/ppermute | solution.py:31
  78.5 3.8 %partials.7 = (bf16[256,1280]{1,0:T(8,128)(2,1)S(1)}, bf16[256,1280]{1,0:T(8,128)(2,1)S(1)}) custom-call(s32[1]{0:T(128)} %bitcast.z_ref, bf16[1024,1024]{1,0:T(8,128)(2,1)S(1)} %dynamic-slice_dynamic-update-slice_fusion.cot_ref, bf16[128,1280]{1,0:T(8,128)(2,1)} %copy-done.4, bf16[128,1280]{1,0:T(8,128)(2,1)} %copy-done.7, bf16[128,1280]{1,0:T(8,128)(2,1)} %copy-done.8, ...), custom_call_target="tpu_custom_call" | custom-call | tf_op jit(solution)/shard_map/partials/pallas_call | solution.py:94
  82.3 1.4 collective-permute-start.10
  83.6 1.5 %collective-permute-start.9 = (bf16[256,1280]{1,0:T(8,128)(2,1)S(1)}, bf16[256,1280]{1,0:T(8,128)(2,1)}, u32[]{:S(2)}, u32[]{:S(2)}) collective-permute-start(bf16[256,1280]{1,0:T(8,128)(2,1)S(1)} %get-tuple-element.17), channel_id=1, source_target_pairs={{0,24},{8,0},{16,8},{24,16},{1,25},{9,1},{17,9},{25,17},{2,26},{10... | collective-permute-start | bytes 1966088 | tf_op jit(solution)/shard_map/ppermute | solution.py:31
  85.2 2.7 %collective-permute-start.17 = (bf16[128,2048]{1,0:T(8,128)(2,1)}, bf16[128,2048]{1,0:T(8,128)(2,1)}, u32[]{:S(2)}, u32[]{:S(2)}) collective-permute-start(bf16[128,2048]{1,0:T(8,128)(2,1)} %collective-permute-done.16.refs_6_), channel_id=1, source_target_pairs={{0,224},{32,0},{64,32},{96,64},{128,96},{160,128},{192,160},{224,1... | collective-permute-start | bytes 1572872 | tf_op jit(solution)/shard_map/ppermute | solution.py:31
  88.7 0.6 fusion.26
  90.0 8.0 %collective-permute-done.15.refs_5_ = bf16[128,2048]{1,0:T(8,128)(2,1)} collective-permute-done((bf16[128,2048]{1,0:T(8,128)(2,1)}, bf16[128,2048]{1,0:T(8,128)(2,1)}, u32[]{:S(2)}, u32[]{:S(2)}) %collective-permute-start.15) | collective-permute-done | bytes 524320 | tf_op jit(solution)/shard_map/ppermute | solution.py:31
  97.9 3.0 %partials.11 = (bf16[256,1024]{1,0:T(8,128)(2,1)S(1)}, bf16[256,1024]{1,0:T(8,128)(2,1)S(1)}) custom-call(s32[1]{0:T(128)} %bitcast.z_ref, bf16[1024,1024]{1,0:T(8,128)(2,1)S(1)} %dynamic-slice_dynamic-update-slice_fusion.cot_ref, bf16[128,2048]{1,0:T(8,128)(2,1)} %copy-done, bf16[128,2048]{1,0:T(8,128)(2,1)} %collective-permute-done.2.refs_1_, ...), custom_call_target="tpu_custom_call" | custom-call | tf_op jit(solution)/shard_map/partials/pallas_call | solution.py:94
  101.0 1.3 collective-permute-start.22
  102.5 3.8 %partials.6 = (bf16[256,1280]{1,0:T(8,128)(2,1)S(1)}, f32[256,1280]{1,0:T(8,128)S(1)}) custom-call(s32[1]{0:T(128)} %bitcast.z_ref, bf16[1024,1024]{1,0:T(8,128)(2,1)S(1)} %dynamic-slice_dynamic-update-slice_fusion.cot_ref, bf16[128,1280]{1,0:T(8,128)(2,1)} %copy-done.4, bf16[128,1280]{1,0:T(8,128)(2,1)} %copy-done.7, bf16[128,1280]{1,0:T(8,128)(2,1)} %copy-done.8, ...), custom_call_target="tpu_custom_call" | custom-call | tf_op jit(solution)/shard_map/partials/pallas_call | solution.py:94
  106.3 1.2 add_convert_fusion.1
  107.7 2.7 %collective-permute-start.12 = (bf16[128,1280]{1,0:T(8,128)(2,1)S(1)}, bf16[128,1280]{1,0:T(8,128)(2,1)S(1)}, u32[]{:S(2)}, u32[]{:S(2)}) collective-permute-start(bf16[128,1280]{1,0:T(8,128)(2,1)S(1)} %get-tuple-element.43), channel_id=1, source_target_pairs={{0,24},{8,0},{16,8},{24,16},{1,25},{9,1},{17,9},{25,17},{2,26},{10... | collective-permute-start | bytes 983048 | tf_op jit(solution)/shard_map/ppermute | solution.py:31
  110.9 3.0 %partials.9 = (bf16[256,1024]{1,0:T(8,128)(2,1)S(1)}, bf16[256,1024]{1,0:T(8,128)(2,1)S(1)}) custom-call(s32[1]{0:T(128)} %bitcast.z_ref, bf16[1024,1024]{1,0:T(8,128)(2,1)S(1)} %dynamic-slice_dynamic-update-slice_fusion.cot_ref, bf16[128,2048]{1,0:T(8,128)(2,1)} %copy-done, bf16[128,2048]{1,0:T(8,128)(2,1)} %collective-permute-done.2.refs_1_, ...), custom_call_target="tpu_custom_call" | custom-call | tf_op jit(solution)/shard_map/partials/pallas_call | solution.py:94
  113.9 1.6 %collective-permute-start.18 = (bf16[256,1024]{1,0:T(8,128)(2,1)S(1)}, bf16[256,1024]{1,0:T(8,128)(2,1)S(1)}, u32[]{:S(2)}, u32[]{:S(2)}) collective-permute-start(bf16[256,1024]{1,0:T(8,128)(2,1)S(1)} %get-tuple-element.21), channel_id=1, source_target_pairs={{0,24},{8,0},{16,8},{24,16},{1,25},{9,1},{17,9},{25,17},{2,26},{10... | collective-permute-start | bytes 1572872 | tf_op jit(solution)/shard_map/ppermute | solution.py:31
  115.5 3.0 %partials.10 = (bf16[256,1024]{1,0:T(8,128)(2,1)S(1)}, f32[256,1024]{1,0:T(8,128)S(1)}) custom-call(s32[1]{0:T(128)} %bitcast.z_ref, bf16[1024,1024]{1,0:T(8,128)(2,1)S(1)} %dynamic-slice_dynamic-update-slice_fusion.cot_ref, bf16[128,2048]{1,0:T(8,128)(2,1)} %copy-done, bf16[128,2048]{1,0:T(8,128)(2,1)} %collective-permute-done.2.refs_1_, ...), custom_call_target="tpu_custom_call" | custom-call | tf_op jit(solution)/shard_map/partials/pallas_call | solution.py:94
  118.6 3.1 %partials.8 = (bf16[256,1024]{1,0:T(8,128)(2,1)S(1)}, f32[256,1024]{1,0:T(8,128)S(1)}) custom-call(s32[1]{0:T(128)} %bitcast.z_ref, bf16[1024,1024]{1,0:T(8,128)(2,1)S(1)} %dynamic-slice_dynamic-update-slice_fusion.cot_ref, bf16[128,2048]{1,0:T(8,128)(2,1)} %copy-done, bf16[128,2048]{1,0:T(8,128)(2,1)} %collective-permute-done.2.refs_1_, ...), custom_call_target="tpu_custom_call" | custom-call | tf_op jit(solution)/shard_map/partials/pallas_call | solution.py:94
  122.3 1.3 slice.148
  123.6 1.0 slice.149
  124.6 2.6 %collective-permute-start.25 = (bf16[128,1024]{1,0:T(8,128)(2,1)S(1)}, bf16[128,1024]{1,0:T(8,128)(2,1)S(1)}, u32[]{:S(2)}, u32[]{:S(2)}) collective-permute-start(bf16[128,1024]{1,0:T(8,128)(2,1)S(1)} %get-tuple-element.45), channel_id=1, source_target_pairs={{0,24},{8,0},{16,8},{24,16},{1,25},{9,1},{17,9},{25,17},{2,26},{10... | collective-permute-start | bytes 786440 | tf_op jit(solution)/shard_map/ppermute | solution.py:31
  127.5 1.1 subtract_convert_fusion.3
  128.6 7.8 %collective-permute-start.26 = (bf16[256,256]{1,0:T(8,128)(2,1)S(1)}, bf16[256,256]{1,0:T(8,128)(2,1)S(1)}, u32[]{:S(2)}, u32[]{:S(2)}) collective-permute-start(bf16[256,256]{1,0:T(8,128)(2,1)S(1)} %slice.162), channel_id=1, source_target_pairs={{0,1},{1,2},{2,3},{3,4},{4,5},{5,6},{6,7},{8,9},{9,10},{10,11},{11... | collective-permute-start | bytes 393224 | tf_op jit(solution)/shard_map/ppermute | solution.py:188
  136.4 2.0 %collective-permute-start.27 = (bf16[256,256]{1,0:T(8,128)(2,1)S(1)}, bf16[256,256]{1,0:T(8,128)(2,1)S(1)}, u32[]{:S(2)}, u32[]{:S(2)}) collective-permute-start(bf16[256,256]{1,0:T(8,128)(2,1)S(1)} %slice.163), channel_id=1, source_target_pairs={{1,0},{2,1},{3,2},{4,3},{5,4},{6,5},{7,6},{9,8},{10,9},{11,10},{12... | collective-permute-start | bytes 393224 | tf_op jit(solution)/shard_map/ppermute | solution.py:189
  139.3 2.5 %collective-permute-start.21 = (bf16[128,1024]{1,0:T(8,128)(2,1)S(1)}, bf16[128,1024]{1,0:T(8,128)(2,1)S(1)}, u32[]{:S(2)}, u32[]{:S(2)}) collective-permute-start(bf16[128,1024]{1,0:T(8,128)(2,1)S(1)} %get-tuple-element.47), channel_id=1, source_target_pairs={{0,24},{8,0},{16,8},{24,16},{1,25},{9,1},{17,9},{25,17},{2,26},{10... | collective-permute-start | bytes 786440 | tf_op jit(solution)/shard_map/ppermute | solution.py:31
  141.9 0.7 collective-permute-done.27
  142.8 3.2 %collective-permute-done.20 = bf16[128,1024]{1,0:T(8,128)(2,1)S(1)} collective-permute-done((bf16[128,1024]{1,0:T(8,128)(2,1)S(1)}, bf16[128,1024]{1,0:T(8,128)(2,1)S(1)}, u32[]{:S(2)}, u32[]{:S(2)}) %collective-permute-start.20) | collective-permute-done | bytes 262176 | tf_op jit(solution)/shard_map/ppermute | solution.py:31
  146.1 1.0 fusion.24
  147.2 0.8 slice-done
  148.1 1.0 fusion.25
  149.2 2.4 %dynamic-slice_select_fusion = bf16[256,3840]{1,0:T(8,128)(2,1)} fusion(bf16[256,4352]{1,0:T(8,128)(2,1)S(1)} %get-tuple-element.30, s32[]{:T(128)S(6)} %select_n.79, pred[3840]{0:T(1024)(128)(4,1)S(1)} %iota_compare_fusion), kind=kLoop, calls=%fused_computation | loop fusion | flops 983040 | bytes 3936004 | tf_op jit(solution)/shard_map/jit(_where)/select_n | solution.py:205
  (94 shorter events, 4.4 us)
Async XLA Ops:
  1.7 32.5 %copy-start = (bf16[128,2048]{1,0:T(8,128)(2,1)}, bf16[128,2048]{1,0:T(8,128)(2,1)S(1)}, u32[]{:S(2)}) copy-start(bf16[128,2048]{1,0:T(8,128)(2,1)S(1)} %slice.114.refs_0_) | copy-start | bytes 1572868
  1.7 30.8 %collective-permute-start.2 = (bf16[128,2048]{1,0:T(8,128)(2,1)S(1)}, bf16[128,2048]{1,0:T(8,128)(2,1)}, u32[]{:S(2)}, u32[]{:S(2)}) collective-permute-start(bf16[128,2048]{1,0:T(8,128)(2,1)S(1)} %slice.114.refs_0_), channel_id=1, source_target_pairs={{0,32},{32,64},{64,96},{96,128},{128,160},{160,192},{192,224},{224... | collective-permute-start | bytes 1572872 | tf_op jit(solution)/shard_map/ppermute | solution.py:31
  4.3 28.3 %collective-permute-start.3 = (bf16[128,2048]{1,0:T(8,128)(2,1)S(1)}, bf16[128,2048]{1,0:T(8,128)(2,1)S(1)}, u32[]{:S(2)}, u32[]{:S(2)}) collective-permute-start(bf16[128,2048]{1,0:T(8,128)(2,1)S(1)} %slice.114.refs_0_), channel_id=1, source_target_pairs={{0,224},{32,0},{64,32},{96,64},{128,96},{160,128},{192,160},{224,1... | collective-permute-start | bytes 1572872 | tf_op jit(solution)/shard_map/ppermute | solution.py:31
  10.0 22.5 %all-to-all-start = ((bf16[16,8,1024]{2,0,1:T(8,128)(2,1)}), bf16[16,8,1024]{2,0,1:T(8,128)(2,1)S(1)}, u32[]{:S(2)}, u32[]{:S(2)}) async-start(bf16[16,8,1024]{2,0,1:T(8,128)(2,1)} %bitcast.13), calls=%async_computation | async-start | bytes 524288 | tf_op jit(solution)/shard_map/all_to_all | solution.py:150
  16.2 1.6 %copy-start.4 = (bf16[128,1280]{1,0:T(8,128)(2,1)}, bf16[128,1280]{1,0:T(8,128)(2,1)S(1)}, u32[]{:S(2)}) copy-start(bf16[128,1280]{1,0:T(8,128)(2,1)S(1)} %pad_maximum_fusion.refs_0_) | copy-start | bytes 983044
  16.2 16.3 %collective-permute-start = (bf16[128,1280]{1,0:T(8,128)(2,1)S(1)}, bf16[128,1280]{1,0:T(8,128)(2,1)S(1)}, u32[]{:S(2)}, u32[]{:S(2)}) collective-permute-start(bf16[128,1280]{1,0:T(8,128)(2,1)S(1)} %pad_maximum_fusion.refs_0_), channel_id=1, source_target_pairs={{0,32},{32,64},{64,96},{96,128},{128,160},{160,192},{192,224},{224... | collective-permute-start | bytes 983048 | tf_op jit(solution)/shard_map/ppermute | solution.py:31
  17.8 14.7 %collective-permute-start.1 = (bf16[128,1280]{1,0:T(8,128)(2,1)S(1)}, bf16[128,1280]{1,0:T(8,128)(2,1)S(1)}, u32[]{:S(2)}, u32[]{:S(2)}) collective-permute-start(bf16[128,1280]{1,0:T(8,128)(2,1)S(1)} %pad_maximum_fusion.refs_0_), channel_id=1, source_target_pairs={{0,224},{32,0},{64,32},{96,64},{128,96},{160,128},{192,160},{224,1... | collective-permute-start | bytes 983048 | tf_op jit(solution)/shard_map/ppermute | solution.py:31
  32.5 7.2 %copy-start.7 = (bf16[128,1280]{1,0:T(8,128)(2,1)}, bf16[128,1280]{1,0:T(8,128)(2,1)S(1)}, u32[]{:S(2)}) copy-start(bf16[128,1280]{1,0:T(8,128)(2,1)S(1)} %collective-permute-done.refs_1_) | copy-start | bytes 983044
  32.5 10.0 %copy-start.8 = (bf16[128,1280]{1,0:T(8,128)(2,1)}, bf16[128,1280]{1,0:T(8,128)(2,1)S(1)}, u32[]{:S(2)}) copy-start(bf16[128,1280]{1,0:T(8,128)(2,1)S(1)} %collective-permute-done.1.refs_2_) | copy-start | bytes 983044
  32.5 7.2 %copy-start.1 = (bf16[128,2048]{1,0:T(8,128)(2,1)}, bf16[128,2048]{1,0:T(8,128)(2,1)S(1)}, u32[]{:S(2)}) copy-start(bf16[128,2048]{1,0:T(8,128)(2,1)S(1)} %collective-permute-done.3.refs_2_) | copy-start | bytes 1572868
  34.2 32.6 %all-to-all-start.1 = ((bf16[8,128,1024]{2,1,0:T(8,128)(2,1)}), bf16[8,128,1024]{2,1,0:T(8,128)(2,1)S(1)}, u32[]{:S(2)}, u32[]{:S(2)}) async-start(bf16[8,128,1024]{2,1,0:T(8,128)(2,1)} %broadcast_in_dim.26), calls=%async_computation.1 | async-start | bytes 4194304 | tf_op jit(solution)/shard_map/all_to_all | solution.py:53
  39.7 10.6 %collective-permute-start.4 = (bf16[128,1280]{1,0:T(8,128)(2,1)S(1)}, bf16[128,1280]{1,0:T(8,128)(2,1)}, u32[]{:S(2)}, u32[]{:S(2)}) collective-permute-start(bf16[128,1280]{1,0:T(8,128)(2,1)S(1)} %collective-permute-done.refs_1_), channel_id=1, source_target_pairs={{0,32},{32,64},{64,96},{96,128},{128,160},{160,192},{192,224},{224... | collective-permute-start | bytes 983048 | tf_op jit(solution)/shard_map/ppermute | solution.py:31
  39.8 24.3 %collective-permute-start.14 = (bf16[128,2048]{1,0:T(8,128)(2,1)S(1)}, bf16[128,2048]{1,0:T(8,128)(2,1)}, u32[]{:S(2)}, u32[]{:S(2)}) collective-permute-start(bf16[128,2048]{1,0:T(8,128)(2,1)S(1)} %collective-permute-done.3.refs_2_), channel_id=1, source_target_pairs={{0,224},{32,0},{64,32},{96,64},{128,96},{160,128},{192,160},{224,1... | collective-permute-start | bytes 1572872 | tf_op jit(solution)/shard_map/ppermute | solution.py:31
  42.5 18.5 %collective-permute-start.5 = (bf16[128,1280]{1,0:T(8,128)(2,1)S(1)}, bf16[128,1280]{1,0:T(8,128)(2,1)}, u32[]{:S(2)}, u32[]{:S(2)}) collective-permute-start(bf16[128,1280]{1,0:T(8,128)(2,1)S(1)} %collective-permute-done.1.refs_2_), channel_id=1, source_target_pairs={{0,224},{32,0},{64,32},{96,64},{128,96},{160,128},{192,160},{224,1... | collective-permute-start | bytes 983048 | tf_op jit(solution)/shard_map/ppermute | solution.py:31
  50.3 13.8 %collective-permute-start.6 = (bf16[128,1280]{1,0:T(8,128)(2,1)}, bf16[128,1280]{1,0:T(8,128)(2,1)S(1)}, u32[]{:S(2)}, u32[]{:S(2)}) collective-permute-start(bf16[128,1280]{1,0:T(8,128)(2,1)} %collective-permute-done.4.refs_3_), channel_id=1, source_target_pairs={{0,32},{32,64},{64,96},{96,128},{128,160},{160,192},{192,224},{224... | collective-permute-start | bytes 983048 | tf_op jit(solution)/shard_map/ppermute | solution.py:31
  50.3 34.8 %collective-permute-start.13 = (bf16[128,2048]{1,0:T(8,128)(2,1)}, bf16[128,2048]{1,0:T(8,128)(2,1)}, u32[]{:S(2)}, u32[]{:S(2)}) collective-permute-start(bf16[128,2048]{1,0:T(8,128)(2,1)} %collective-permute-done.2.refs_1_), channel_id=1, source_target_pairs={{0,32},{32,64},{64,96},{96,128},{128,160},{160,192},{192,224},{224... | collective-permute-start | bytes 1572872 | tf_op jit(solution)/shard_map/ppermute | solution.py:31
  61.0 10.2 %collective-permute-start.7 = (bf16[128,1280]{1,0:T(8,128)(2,1)}, bf16[128,1280]{1,0:T(8,128)(2,1)S(1)}, u32[]{:S(2)}, u32[]{:S(2)}) collective-permute-start(bf16[128,1280]{1,0:T(8,128)(2,1)} %collective-permute-done.5.refs_4_), channel_id=1, source_target_pairs={{0,224},{32,0},{64,32},{96,64},{128,96},{160,128},{192,160},{224,1... | collective-permute-start | bytes 983048 | tf_op jit(solution)/shard_map/ppermute | solution.py:31
  64.1 2.9 %copy-start.9 = (bf16[128,1280]{1,0:T(8,128)(2,1)}, bf16[128,1280]{1,0:T(8,128)(2,1)S(1)}, u32[]{:S(2)}) copy-start(bf16[128,1280]{1,0:T(8,128)(2,1)S(1)} %collective-permute-done.6.refs_5_) | copy-start | bytes 983044
  64.1 14.4 %collective-permute-start.8 = (bf16[128,1280]{1,0:T(8,128)(2,1)S(1)}, bf16[128,1280]{1,0:T(8,128)(2,1)}, u32[]{:S(2)}, u32[]{:S(2)}) collective-permute-start(bf16[128,1280]{1,0:T(8,128)(2,1)S(1)} %collective-permute-done.6.refs_5_), channel_id=1, source_target_pairs={{0,32},{32,64},{64,96},{96,128},{128,160},{160,192},{192,224},{224... | collective-permute-start | bytes 983048 | tf_op jit(solution)/shard_map/ppermute | solution.py:31
  64.1 21.1 %collective-permute-start.16 = (bf16[128,2048]{1,0:T(8,128)(2,1)}, bf16[128,2048]{1,0:T(8,128)(2,1)}, u32[]{:S(2)}, u32[]{:S(2)}) collective-permute-start(bf16[128,2048]{1,0:T(8,128)(2,1)} %collective-permute-done.14.refs_4_), channel_id=1, source_target_pairs={{0,224},{32,0},{64,32},{96,64},{128,96},{160,128},{192,160},{224,1... | collective-permute-start | bytes 1572872 | tf_op jit(solution)/shard_map/ppermute | solution.py:31
  71.2 7.3 %copy-start.10 = (bf16[128,1280]{1,0:T(8,128)(2,1)}, bf16[128,1280]{1,0:T(8,128)(2,1)S(1)}, u32[]{:S(2)}) copy-start(bf16[128,1280]{1,0:T(8,128)(2,1)S(1)} %collective-permute-done.7.refs_6_) | copy-start | bytes 983044
  78.5 10.2 %copy-start.15 = (s32[8]{0:T(128)S(1)}, s32[8]{0:T(128)}, u32[]{:S(2)}) copy-start(s32[8]{0:T(128)} %param.12) | copy-start | bytes 100
  82.3 24.1 %collective-permute-start.10 = (bf16[256,1280]{1,0:T(8,128)(2,1)S(1)}, bf16[256,1280]{1,0:T(8,128)(2,1)}, u32[]{:S(2)}, u32[]{:S(2)}) collective-permute-start(bf16[256,1280]{1,0:T(8,128)(2,1)S(1)} %get-tuple-element.18), channel_id=1, source_target_pairs={{0,8},{8,16},{16,24},{24,0},{1,9},{9,17},{17,25},{25,1},{2,10},{10... | collective-permute-start | bytes 1966088 | tf_op jit(solution)/shard_map/ppermute | solution.py:31
  83.6 22.7 %collective-permute-start.9 = (bf16[256,1280]{1,0:T(8,128)(2,1)S(1)}, bf16[256,1280]{1,0:T(8,128)(2,1)}, u32[]{:S(2)}, u32[]{:S(2)}) collective-permute-start(bf16[256,1280]{1,0:T(8,128)(2,1)S(1)} %get-tuple-element.17), channel_id=1, source_target_pairs={{0,24},{8,0},{16,8},{24,16},{1,25},{9,1},{17,9},{25,17},{2,26},{10... | collective-permute-start | bytes 1966088 | tf_op jit(solution)/shard_map/ppermute | solution.py:31
  85.2 12.8 %collective-permute-start.15 = (bf16[128,2048]{1,0:T(8,128)(2,1)}, bf16[128,2048]{1,0:T(8,128)(2,1)}, u32[]{:S(2)}, u32[]{:S(2)}) collective-permute-start(bf16[128,2048]{1,0:T(8,128)(2,1)} %collective-permute-done.13.refs_3_), channel_id=1, source_target_pairs={{0,32},{32,64},{64,96},{96,128},{128,160},{160,192},{192,224},{224... | collective-permute-start | bytes 1572872 | tf_op jit(solution)/shard_map/ppermute | solution.py:31
  85.2 12.8 %collective-permute-start.17 = (bf16[128,2048]{1,0:T(8,128)(2,1)}, bf16[128,2048]{1,0:T(8,128)(2,1)}, u32[]{:S(2)}, u32[]{:S(2)}) collective-permute-start(bf16[128,2048]{1,0:T(8,128)(2,1)} %collective-permute-done.16.refs_6_), channel_id=1, source_target_pairs={{0,224},{32,0},{64,32},{96,64},{128,96},{160,128},{192,160},{224,1... | collective-permute-start | bytes 1572872 | tf_op jit(solution)/shard_map/ppermute | solution.py:31
  101.0 20.6 %collective-permute-start.22 = (bf16[256,1024]{1,0:T(8,128)(2,1)S(1)}, bf16[256,1024]{1,0:T(8,128)(2,1)S(1)}, u32[]{:S(2)}, u32[]{:S(2)}) collective-permute-start(bf16[256,1024]{1,0:T(8,128)(2,1)S(1)} %get-tuple-element.25), channel_id=1, source_target_pairs={{0,24},{8,0},{16,8},{24,16},{1,25},{9,1},{17,9},{25,17},{2,26},{10... | collective-permute-start | bytes 1572872 | tf_op jit(solution)/shard_map/ppermute | solution.py:31
  102.3 19.6 %collective-permute-start.23 = (bf16[256,1024]{1,0:T(8,128)(2,1)S(1)}, bf16[256,1024]{1,0:T(8,128)(2,1)S(1)}, u32[]{:S(2)}, u32[]{:S(2)}) collective-permute-start(bf16[256,1024]{1,0:T(8,128)(2,1)S(1)} %get-tuple-element.26), channel_id=1, source_target_pairs={{0,8},{8,16},{16,24},{24,0},{1,9},{9,17},{17,25},{25,1},{2,10},{10... | collective-permute-start | bytes 1572872 | tf_op jit(solution)/shard_map/ppermute | solution.py:31
  107.6 17.0 %collective-permute-start.11 = (bf16[128,1280]{1,0:T(8,128)(2,1)S(1)}, bf16[128,1280]{1,0:T(8,128)(2,1)S(1)}, u32[]{:S(2)}, u32[]{:S(2)}) collective-permute-start(bf16[128,1280]{1,0:T(8,128)(2,1)S(1)} %get-tuple-element.42), channel_id=1, source_target_pairs={{0,8},{8,16},{16,24},{24,0},{1,9},{9,17},{17,25},{25,1},{2,10},{10... | collective-permute-start | bytes 983048 | tf_op jit(solution)/shard_map/ppermute | solution.py:31
  107.7 19.5 %collective-permute-start.12 = (bf16[128,1280]{1,0:T(8,128)(2,1)S(1)}, bf16[128,1280]{1,0:T(8,128)(2,1)S(1)}, u32[]{:S(2)}, u32[]{:S(2)}) collective-permute-start(bf16[128,1280]{1,0:T(8,128)(2,1)S(1)} %get-tuple-element.43), channel_id=1, source_target_pairs={{0,24},{8,0},{16,8},{24,16},{1,25},{9,1},{17,9},{25,17},{2,26},{10... | collective-permute-start | bytes 983048 | tf_op jit(solution)/shard_map/ppermute | solution.py:31
  113.9 22.4 %collective-permute-start.18 = (bf16[256,1024]{1,0:T(8,128)(2,1)S(1)}, bf16[256,1024]{1,0:T(8,128)(2,1)S(1)}, u32[]{:S(2)}, u32[]{:S(2)}) collective-permute-start(bf16[256,1024]{1,0:T(8,128)(2,1)S(1)} %get-tuple-element.21), channel_id=1, source_target_pairs={{0,24},{8,0},{16,8},{24,16},{1,25},{9,1},{17,9},{25,17},{2,26},{10... | collective-permute-start | bytes 1572872 | tf_op jit(solution)/shard_map/ppermute | solution.py:31
  121.6 17.1 %copy-start.11 = (bf16[256,1024]{1,0:T(8,128)(2,1)}, bf16[256,1024]{1,0:T(8,128)(2,1)S(1)}, u32[]{:S(2)}) copy-start(bf16[256,1024]{1,0:T(8,128)(2,1)S(1)} %collective-permute-done.22) | copy-start | bytes 1572868
  121.6 16.7 %collective-permute-start.19 = (bf16[256,1024]{1,0:T(8,128)(2,1)S(1)}, bf16[256,1024]{1,0:T(8,128)(2,1)S(1)}, u32[]{:S(2)}, u32[]{:S(2)}) collective-permute-start(bf16[256,1024]{1,0:T(8,128)(2,1)S(1)} %get-tuple-element.22), channel_id=1, source_target_pairs={{0,8},{8,16},{16,24},{24,0},{1,9},{9,17},{17,25},{25,1},{2,10},{10... | collective-permute-start | bytes 1572872 | tf_op jit(solution)/shard_map/ppermute | solution.py:31
  121.9 16.8 %copy-start.12 = (bf16[256,1024]{1,0:T(8,128)(2,1)}, bf16[256,1024]{1,0:T(8,128)(2,1)S(1)}, u32[]{:S(2)}) copy-start(bf16[256,1024]{1,0:T(8,128)(2,1)S(1)} %collective-permute-done.23) | copy-start | bytes 1572868
  121.9 5.5 %copy-start.6 = (bf16[256,3328]{1,0:T(8,128)(2,1)S(1)}, bf16[256,3328]{1,0:T(8,128)(2,1)}, u32[]{:S(2)}) copy-start(bf16[256,3328]{1,0:T(8,128)(2,1)} %param.10) | copy-start | bytes 5111812
  122.1 25.1 %collective-permute-start.24 = (bf16[128,1024]{1,0:T(8,128)(2,1)S(1)}, bf16[128,1024]{1,0:T(8,128)(2,1)S(1)}, u32[]{:S(2)}, u32[]{:S(2)}) collective-permute-start(bf16[128,1024]{1,0:T(8,128)(2,1)S(1)} %get-tuple-element.44), channel_id=1, source_target_pairs={{0,8},{8,16},{16,24},{24,0},{1,9},{9,17},{17,25},{25,1},{2,10},{10... | collective-permute-start | bytes 786440 | tf_op jit(solution)/shard_map/ppermute | solution.py:31
  122.3 5.2 %copy-start.5 = (bf16[256,3328]{1,0:T(8,128)(2,1)S(1)}, bf16[256,3328]{1,0:T(8,128)(2,1)}, u32[]{:S(2)}) copy-start(bf16[256,3328]{1,0:T(8,128)(2,1)} %param.11) | copy-start | bytes 5111812
  124.6 2.9 %copy-start.3 = (f32[256,3328]{1,0:T(8,128)S(1)}, f32[256,3328]{1,0:T(8,128)}, u32[]{:S(2)}) copy-start(f32[256,3328]{1,0:T(8,128)} %param.9) | copy-start | bytes 10223620
  124.6 22.6 %collective-permute-start.25 = (bf16[128,1024]{1,0:T(8,128)(2,1)S(1)}, bf16[128,1024]{1,0:T(8,128)(2,1)S(1)}, u32[]{:S(2)}, u32[]{:S(2)}) collective-permute-start(bf16[128,1024]{1,0:T(8,128)(2,1)S(1)} %get-tuple-element.45), channel_id=1, source_target_pairs={{0,24},{8,0},{16,8},{24,16},{1,25},{9,1},{17,9},{25,17},{2,26},{10... | collective-permute-start | bytes 786440 | tf_op jit(solution)/shard_map/ppermute | solution.py:31
  128.6 10.7 %collective-permute-start.26 = (bf16[256,256]{1,0:T(8,128)(2,1)S(1)}, bf16[256,256]{1,0:T(8,128)(2,1)S(1)}, u32[]{:S(2)}, u32[]{:S(2)}) collective-permute-start(bf16[256,256]{1,0:T(8,128)(2,1)S(1)} %slice.162), channel_id=1, source_target_pairs={{0,1},{1,2},{2,3},{3,4},{4,5},{5,6},{6,7},{8,9},{9,10},{10,11},{11... | collective-permute-start | bytes 393224 | tf_op jit(solution)/shard_map/ppermute | solution.py:188
  136.4 2.6 %copy-start.13 = (bf16[256,1024]{1,0:T(8,128)(2,1)}, bf16[256,1024]{1,0:T(8,128)(2,1)S(1)}, u32[]{:S(2)}) copy-start(bf16[256,1024]{1,0:T(8,128)(2,1)S(1)} %collective-permute-done.18) | copy-start | bytes 1572868
  136.4 6.3 %collective-permute-start.27 = (bf16[256,256]{1,0:T(8,128)(2,1)S(1)}, bf16[256,256]{1,0:T(8,128)(2,1)S(1)}, u32[]{:S(2)}, u32[]{:S(2)}) collective-permute-start(bf16[256,256]{1,0:T(8,128)(2,1)S(1)} %slice.163), channel_id=1, source_target_pairs={{1,0},{2,1},{3,2},{4,3},{5,4},{6,5},{7,6},{9,8},{10,9},{11,10},{12... | collective-permute-start | bytes 393224 | tf_op jit(solution)/shard_map/ppermute | solution.py:189
  138.6 7.4 %collective-permute-start.20 = (bf16[128,1024]{1,0:T(8,128)(2,1)S(1)}, bf16[128,1024]{1,0:T(8,128)(2,1)S(1)}, u32[]{:S(2)}, u32[]{:S(2)}) collective-permute-start(bf16[128,1024]{1,0:T(8,128)(2,1)S(1)} %get-tuple-element.46), channel_id=1, source_target_pairs={{0,8},{8,16},{16,24},{24,0},{1,9},{9,17},{17,25},{25,1},{2,10},{10... | collective-permute-start | bytes 786440 | tf_op jit(solution)/shard_map/ppermute | solution.py:31
  139.2 6.9 %slice-start.2 = ((bf16[256,1024]{1,0:T(8,128)(2,1)}), bf16[128,1024]{1,0:T(8,128)(2,1)S(1)}, s32[]{:S(2)}) async-start(bf16[256,1024]{1,0:T(8,128)(2,1)} %copy-done.13), calls=%async_computation.4 | async-start | bytes 524288 | tf_op jit(solution)/shard_map/slice | solution.py:125
  139.2 6.8 %slice-start.3 = ((bf16[256,1024]{1,0:T(8,128)(2,1)}), bf16[128,1024]{1,0:T(8,128)(2,1)S(1)}, s32[]{:S(2)}) async-start(bf16[256,1024]{1,0:T(8,128)(2,1)} %copy-done.14), calls=%async_computation.5 | async-start | bytes 524288 | tf_op jit(solution)/shard_map/slice | solution.py:125
  139.3 6.8 %collective-permute-start.21 = (bf16[128,1024]{1,0:T(8,128)(2,1)S(1)}, bf16[128,1024]{1,0:T(8,128)(2,1)S(1)}, u32[]{:S(2)}, u32[]{:S(2)}) collective-permute-start(bf16[128,1024]{1,0:T(8,128)(2,1)S(1)} %get-tuple-element.47), channel_id=1, source_target_pairs={{0,24},{8,0},{16,8},{24,16},{1,25},{9,1},{17,9},{25,17},{2,26},{10... | collective-permute-start | bytes 786440 | tf_op jit(solution)/shard_map/ppermute | solution.py:31
  147.1 1.0 slice-start.1
  149.2 2.4 %copy-start.2 = (f32[256,3328]{1,0:T(8,128)}, f32[256,3328]{1,0:T(8,128)S(1)}, u32[]{:S(2)}) copy-start(f32[256,3328]{1,0:T(8,128)S(1)} %constant_dynamic-update-slice_fusion.3) | copy-start | bytes 10223620
  (2 other events, 1.7 us)
